TPU v7x, 32 devices: a whole 2x2x4 slice. The times are simulated.
32 devices in a mesh: view: 4 (over x, core), gy: 2 (over y), gz: 4 (over z).
Axes of the slice: x: 2, y: 2, z: 4, core: 2. Of those that a mesh axis runs over, the one named last changes fastest.
Arguments:
- estimate: float32 [16, 128, 1024], P('view', 'gy', 'gz'), may hold values from 0.5 to 2
- view_data: bfloat16 [8, 16, 128, 1024], P('view', None, 'gy', 'gz'), may hold values from 0.25 to 2
- block_scales: float32 [8, 4, 16], P('view', 'gy', 'gz'), may hold values from 0.5 to 2
- block_flags: int32 [8, 4, 16], P('view', 'gy', 'gz'), may hold values 0 or 1
- profile: float32 [8, 3, 33], P('view'), may hold values from 0.05 to 1
- supports: int32 [8, 3], P('view'), may hold values from 1 to 16, as said below
Outputs:
- refined: float32 [16, 128, 1024], P('view', 'gy', 'gz')
Inputs may be any that keep to these rules, and one draw needn't show every extreme that they name: supports[v] holds view v's half-widths along x, y and z: along x 1 to 6, along y and z 1 to 16; some view has 6 along x, some view 16 along y and some view 16 along z. block_flags[v, b, c] is 1 where view v's data in the block of 32 x 64 cells (b, c) are valid.
All inputs are finite; a program needn't handle non-finite values.
Results may differ from a plain program's by a relative error of at most 0.0003.
Values sent between devices are 32-bit elements; how exact they have to be, the bound alone decides.
A program may use at most 64 MiB of HBM per device.

v0:
```python
import jax
import jax.numpy as jnp
from jax import lax
from jax.sharding import PartitionSpec as P

BY = 32
BZ = 64
ITERS = 2


def extended(x, sides, width):
    for axis, dim in sides:
        size, length = (lax.axis_size(axis), x.shape[dim])
        up = [(i, (i + 1) % size) for i in range(size - 1)]
        down = [(j, i) for i, j in up]
        last = lax.slice_in_dim(x, length - width, length, axis=dim)
        first = lax.slice_in_dim(x, 0, width, axis=dim)
        before = lax.ppermute(last, axis, up)
        after = lax.ppermute(first, axis, down)
        x = jnp.concatenate([before, x, after], axis=dim)
    return x


def band_matrix(tap_table, row_count, col_count, offset):
    row_index = lax.broadcasted_iota(jnp.int32, (row_count, col_count), 0)
    col_index = lax.broadcasted_iota(jnp.int32, (row_count, col_count), 1)
    lag_index = row_index - col_index + offset

    def place_tap(tap_index, summed):
        return jnp.where(lag_index == tap_index, tap_table[tap_index], summed)

    return lax.fori_loop(
        0, tap_table.shape[0], place_tap, jnp.zeros((row_count, col_count), jnp.float32)
    )


def band_stack(kernels, row_count, col_count, offset):
    return jax.vmap(lambda tap_table: band_matrix(tap_table, row_count, col_count, offset))(kernels)


def kernel_table(profile, supports):
    tap_count = profile.shape[-1]
    distance = jnp.abs(jnp.arange(tap_count, dtype=jnp.int32) - (tap_count - 1) // 2)
    inside = distance[None, None, :] <= supports[:, :, None]
    masked = jnp.where(inside, profile, 0.0)
    return masked / jnp.sum(masked, axis=-1, keepdims=True)


def build_mats(kernels, planes, half_width):
    plane_mats = band_stack(kernels[:, 0], planes, planes, half_width)
    row_bands = band_stack(kernels[:, 1], 4 * half_width, 2 * half_width, 0)
    col_bands = band_stack(kernels[:, 2], 4 * half_width, 2 * half_width, 0)
    return (plane_mats, row_bands, col_bands)


def axis_blur(field, bands, axis):
    width = bands.shape[2]
    moved = jnp.moveaxis(field, axis, -1)
    count = moved.shape[-1] // width - 1
    tiles = moved.reshape(moved.shape[:-1] + (count + 1, width))
    early = jnp.einsum(
        "v...bj,vji->v...bi", tiles[..., :-1, :], bands[:, :width], precision=lax.Precision.HIGHEST
    )
    later = jnp.einsum(
        "v...bj,vji->v...bi", tiles[..., 1:, :], bands[:, width:], precision=lax.Precision.HIGHEST
    )
    joined = (early + later).reshape(moved.shape[:-1] + (count * width,))
    return jnp.moveaxis(joined, -1, axis)


def mix_planes(field, plane_mats):
    return jnp.einsum("vjyz,vji->viyz", field, plane_mats, precision=lax.Precision.HIGHEST)


def forward_blur(current, mats, half_width, local_views):
    plane_mats, row_bands, col_bands = mats
    padded = extended(current, (("gy", 1),), half_width)
    stacked = jnp.broadcast_to(padded[None], (local_views,) + padded.shape)
    along_rows = axis_blur(stacked, row_bands, 2)
    along_rows = extended(along_rows, (("gz", 3),), half_width)
    return mix_planes(axis_blur(along_rows, col_bands, 3), plane_mats)


def back_blur(ratios, mats, half_width):
    plane_mats, row_bands, col_bands = mats
    padded = extended(ratios, (("gy", 2),), half_width)
    along_rows = axis_blur(padded, row_bands, 2)
    along_rows = extended(along_rows, (("gz", 3),), half_width)
    return mix_planes(axis_blur(along_rows, col_bands, 3), plane_mats)


def per_device(estimate, view_data, block_scales, block_flags, profile, supports):
    local_views, planes, rows_y, rows_z = view_data.shape
    half_width = (profile.shape[2] - 1) // 2
    view_total = local_views * lax.axis_size("view")
    forward = kernel_table(profile, supports)
    backward = forward[:, :, ::-1]
    forward_mats = build_mats(forward, planes, half_width)
    backward_mats = build_mats(backward, planes, half_width)
    block_count = rows_z // BZ
    cell_block = lax.broadcasted_iota(jnp.int32, (block_count, rows_z), 1) // BZ
    block_number = lax.broadcasted_iota(jnp.int32, (block_count, rows_z), 0)
    spread_cols = (cell_block == block_number).astype(jnp.float32)
    scale_rows = jnp.einsum(
        "vbc,cz->vbz", block_scales, spread_cols, precision=lax.Precision.HIGHEST
    )
    valid_rows = jnp.einsum(
        "vbc,cz->vbz", block_flags.astype(jnp.float32), spread_cols, precision=lax.Precision.HIGHEST
    )
    split_shape = (local_views, planes, rows_y // BY, BY, rows_z)
    measured = view_data.astype(jnp.float32).reshape(split_shape) * scale_rows[:, None, :, None, :]
    valid_cells = valid_rows[:, None, :, None, :] > 0.5
    owned_planes = estimate
    current = lax.all_gather(estimate, "view", axis=0, tiled=True)
    for iteration in range(ITERS):
        blurred = forward_blur(current, forward_mats, half_width, local_views)
        ratios = jnp.where(valid_cells, measured / blurred.reshape(split_shape), 1.0).reshape(
            blurred.shape
        )
        summed = jnp.sum(back_blur(ratios, backward_mats, half_width), axis=0)
        owner_sum = lax.psum_scatter(summed, "view", scatter_dimension=0, tiled=True)
        owned_planes = owned_planes * owner_sum / view_total
        if iteration + 1 < ITERS:
            current = lax.all_gather(owned_planes, "view", axis=0, tiled=True)
    return owned_planes


def solution(mesh):
    placed = (
        P("view", "gy", "gz"),
        P("view", None, "gy", "gz"),
        P("view", "gy", "gz"),
        P("view", "gy", "gz"),
        P("view", None, None),
        P("view", None),
    )
    return jax.shard_map(
        per_device, mesh=mesh, in_specs=placed, out_specs=P("view", "gy", "gz"), check_vma=False
    )
```

profile of v0, /device:TPU:0, one launch (start us, length us, event | category | flops | bytes accessed | tf_op | source)
XLA Modules:
  0.0 326.6 jit_solution(14267828636494118689)
XLA Ops:
  10.2 3.4 %while.95 = (s32[]{:T(128)}, f32[2,64,32]{2,1,0:T(8,128)S(1)}, f32[2,33]{0,1:T(8,128)S(1)}, s32[]{:T(128)}, s32[]{:T(128)}) while((s32[]{:T(128)}, f32[2,64,32]{2,1,0:T(8,128)S(1)}, f32[2,33]{0,1:T(8,128)S(1)}, s32[]{:T(128)}, s32[]{:T(128)}) %tuple.237), condition=%wide.region_12.13_spmd.clone, body=%wide.region_11.12_spmd.clone.sunk | while | flops 12291 | bytes 36975 | solution.py:32
  13.7 3.4 %while.93 = (s32[]{:T(128)}, f32[2,64,32]{2,1,0:T(8,128)S(1)}, f32[2,33]{0,1:T(8,128)S(1)}, s32[]{:T(128)}, s32[]{:T(128)}) while((s32[]{:T(128)}, f32[2,64,32]{2,1,0:T(8,128)S(1)}, f32[2,33]{0,1:T(8,128)S(1)}, s32[]{:T(128)}, s32[]{:T(128)}) %tuple.228), condition=%wide.region_8.9_spmd.clone, body=%wide.region_7.8_spmd.clone.sunk | while | flops 12291 | bytes 36975 | solution.py:32
  17.1 3.4 %while.92 = (s32[]{:T(128)}, f32[2,64,32]{2,1,0:T(8,128)S(1)}, f32[2,33]{0,1:T(8,128)S(1)}, s32[]{:T(128)}, s32[]{:T(128)}) while((s32[]{:T(128)}, f32[2,64,32]{2,1,0:T(8,128)S(1)}, f32[2,33]{0,1:T(8,128)S(1)}, s32[]{:T(128)}, s32[]{:T(128)}) %tuple.225), condition=%wide.region_6.7_spmd.clone, body=%wide.region_5.6_spmd.clone.sunk | while | flops 12291 | bytes 36975 | solution.py:32
  20.5 3.0 while.91
  23.5 4.8 %all-gather.3.cloned.1.call-done = f32[16,64,256]{2,1,0:T(8,128)} async-done(((f32[4,64,256]{2,1,0:T(8,128)}), f32[16,64,256]{2,1,0:T(8,128)}) %all-gather.3.cloned.1.call-update) | async-done | bytes 1048592 | tf_op jit(solution)/shard_map/all_gather | solution.py:114
  29.4 3.4 %collective-permute-start = (f32[16,16,256]{2,1,0:T(8,128)S(1)}, f32[16,16,256]{2,1,0:T(8,128)S(1)}, u32[]{:S(2)}, u32[]{:S(2)}) collective-permute-start(f32[16,16,256]{2,1,0:T(8,128)S(1)} %get-tuple-element.725), channel_id=1, source_target_pairs={{0,4},{1,5},{2,6},{3,7},{8,12},{9,13},{10,14},{11,15},{16,20},{17,... | collective-permute-start | bytes 786440 | tf_op jit(solution)/shard_map/ppermute | solution.py:18
  34.7 4.1 %collective-permute-done = f32[16,16,256]{2,1,0:T(8,128)S(1)} collective-permute-done((f32[16,16,256]{2,1,0:T(8,128)S(1)}, f32[16,16,256]{2,1,0:T(8,128)S(1)}, u32[]{:S(2)}, u32[]{:S(2)}) %collective-permute-start) | collective-permute-done | bytes 262176 | tf_op jit(solution)/shard_map/ppermute | solution.py:18
  38.8 4.1 %collective-permute-done.1 = f32[16,16,256]{2,1,0:T(8,128)S(1)} collective-permute-done((f32[16,16,256]{2,1,0:T(8,128)S(1)}, f32[16,16,256]{2,1,0:T(8,128)S(1)}, u32[]{:S(2)}, u32[]{:S(2)}) %collective-permute-start.1) | collective-permute-done | bytes 262176 | tf_op jit(solution)/shard_map/ppermute | solution.py:19
  44.7 1.9 fusion.28
  46.7 2.1 convolution_add_fusion.5
  48.8 2.8 copy.49
  52.6 3.4 %collective-permute-start.2 = (f32[2,16,64,16]{2,3,1,0:T(8,128)S(1)}, f32[2,16,64,16]{2,3,1,0:T(8,128)S(1)}, u32[]{:S(2)}, u32[]{:S(2)}) collective-permute-start(f32[2,16,64,16]{2,3,1,0:T(8,128)S(1)} %get-tuple-element.713), channel_id=1, source_target_pairs={{0,1},{1,2},{2,3},{4,5},{5,6},{6,7},{8,9},{9,10},{10,11},{12,13},{... | collective-permute-start | bytes 393224 | tf_op jit(solution)/shard_map/ppermute | solution.py:18
  57.6 3.1 collective-permute-done.2
  60.8 4.1 %collective-permute-done.3 = f32[2,16,64,16]{2,3,1,0:T(8,128)S(1)} collective-permute-done((f32[2,16,64,16]{2,3,1,0:T(8,128)S(1)}, f32[2,16,64,16]{2,3,1,0:T(8,128)S(1)}, u32[]{:S(2)}, u32[]{:S(2)}) %collective-permute-start.3) | collective-permute-done | bytes 131104 | tf_op jit(solution)/shard_map/ppermute | solution.py:19
  64.9 2.8 pad_maximum_fusion
  67.7 3.7 %fusion.30 = f32[2,16,64,8,32]{2,4,3,1,0:T(8,128)S(1)} fusion(f32[2,16,64,9,32]{2,4,3,1,0:T(8,128)S(1)} %bitcast.160, f32[2,64,32]{1,2,0:T(8,128)S(1)} %copy.51), kind=kOutput, calls=%fused_computation.69 | convolution fusion | flops 201326592 | bytes 4472832 | tf_op jit(solution)/shard_map/v...bj,vji->v...bi/dot_general | solution.py:64
  71.4 5.1 %convolution_add_fusion.3 = f32[2,16,64,8,32]{2,4,3,1,0:T(8,128)} fusion(f32[2,16,64,8,32]{2,4,3,1,0:T(8,128)S(1)} %fusion.30, f32[2,16,64,9,32]{2,4,3,1,0:T(8,128)S(1)} %bitcast.161, f32[2,64,32]{1,2,0:T(8,128)S(1)} %copy.51), kind=kOutput, calls=%fused_computation.33 | convolution fusion | flops 201850880 | bytes 6569984 | tf_op jit(solution)/shard_map/v...bj,vji->v...bi/dot_general | solution.py:61
  76.5 4.2 %copy.54 = f32[2,16,64,256]{3,1,2,0:T(8,128)} copy(f32[2,16,64,256]{2,3,1,0:T(8,128)} %bitcast.180) | data formatting | bytes 4194304 | tf_op jit(solution)/shard_map/reshape | solution.py:67
  80.8 4.5 %divide_select_fusion.1 = f32[2,16,64,256]{3,1,2,0:T(8,128)S(1)} fusion(f32[2,16,64,256]{3,1,2,0:T(8,128)} %copy.54, f32[2,64,256]{2,1,0:T(8,128)S(1)} %bitcast.186, pred[2,64,256]{2,1,0:T(8,128)(4,1)S(1)} %bitcast.188, bf16[2,16,64,256]{3,2,1,0:T(8,128)(2,1)} %param.19, f32[2,16,16]{2,1,0:T(8,128)S(1)} %get-tuple-element.480), kind=kOutput, calls=%fused_computation.43 | convolution fusion | flops 102760448 | bytes 5408768 | tf_op jit(solution)/shard_map/vjyz,vji->viyz/dot_general | solution.py:72
  89.3 3.4 %while.94 = (s32[]{:T(128)}, f32[2,64,32]{2,1,0:T(8,128)S(1)}, f32[2,33]{0,1:T(8,128)S(1)}, s32[]{:T(128)}, s32[]{:T(128)}) while((s32[]{:T(128)}, f32[2,64,32]{2,1,0:T(8,128)S(1)}, f32[2,33]{0,1:T(8,128)S(1)}, s32[]{:T(128)}, s32[]{:T(128)}) %tuple.234), condition=%wide.region_10.11_spmd.clone, body=%wide.region_9.10_spmd.clone.sunk | while | flops 12291 | bytes 36975 | solution.py:32
  93.0 4.4 %collective-permute-done.4 = f32[2,16,16,256]{3,1,2,0:T(8,128)S(1)} collective-permute-done((f32[2,16,16,256]{3,1,2,0:T(8,128)}, f32[2,16,16,256]{3,1,2,0:T(8,128)S(1)}, u32[]{:S(2)}, u32[]{:S(2)}) %collective-permute-start.4) | collective-permute-done | bytes 524320 | tf_op jit(solution)/shard_map/ppermute | solution.py:18
  97.5 4.1 %collective-permute-done.5 = f32[2,16,16,256]{3,1,2,0:T(8,128)} collective-permute-done((f32[2,16,16,256]{3,1,2,0:T(8,128)}, f32[2,16,16,256]{3,1,2,0:T(8,128)}, u32[]{:S(2)}, u32[]{:S(2)}) %collective-permute-start.5) | collective-permute-done | bytes 524320 | tf_op jit(solution)/shard_map/ppermute | solution.py:19
  103.7 3.2 fusion.16
  106.9 3.4 %fusion.20 = f32[2,16,256,2,32]{2,4,3,1,0:T(8,128)S(1)} fusion(f32[2,16,256,2,32]{2,4,3,1,0:T(8,128)S(1)} %fusion.16, f32[2,16,256,2,32]{2,1,4,3,0:T(8,128)S(1)} %get-tuple-element.717, f32[2,64,32]{1,2,0:T(8,128)S(1)} %copy.57), kind=kOutput, calls=%fused_computation.45 | convolution fusion | flops 201850880 | bytes 6307840 | tf_op jit(solution)/shard_map/v...bj,vji->v...bi/dot_general | solution.py:61
  110.3 2.8 copy.60
  114.2 3.4 %collective-permute-start.6 = (f32[2,16,64,16]{2,3,1,0:T(8,128)S(1)}, f32[2,16,64,16]{2,3,1,0:T(8,128)S(1)}, u32[]{:S(2)}, u32[]{:S(2)}) collective-permute-start(f32[2,16,64,16]{2,3,1,0:T(8,128)S(1)} %get-tuple-element.711), channel_id=1, source_target_pairs={{0,1},{1,2},{2,3},{4,5},{5,6},{6,7},{8,9},{9,10},{10,11},{12,13},{... | collective-permute-start | bytes 393224 | tf_op jit(solution)/shard_map/ppermute | solution.py:18
  117.6 1.8 collective-permute-start.7
  119.3 3.1 while.90
  122.5 3.4 %collective-permute-done.7 = f32[2,16,64,16]{2,3,1,0:T(8,128)S(1)} collective-permute-done((f32[2,16,64,16]{2,3,1,0:T(8,128)S(1)}, f32[2,16,64,16]{2,3,1,0:T(8,128)S(1)}, u32[]{:S(2)}, u32[]{:S(2)}) %collective-permute-start.7) | collective-permute-done | bytes 131104 | tf_op jit(solution)/shard_map/ppermute | solution.py:19
  125.8 2.8 pad_maximum_fusion.1
  128.6 3.7 %fusion.32 = f32[2,16,64,8,32]{2,4,3,1,0:T(8,128)S(1)} fusion(f32[2,16,64,9,32]{2,4,3,1,0:T(8,128)S(1)} %bitcast.162, f32[2,64,32]{1,2,0:T(8,128)S(1)} %copy.62), kind=kOutput, calls=%fused_computation.71 | convolution fusion | flops 201326592 | bytes 4472832 | tf_op jit(solution)/shard_map/v...bj,vji->v...bi/dot_general | solution.py:64
  132.3 5.1 %convolution_add_fusion.2 = f32[2,16,64,8,32]{2,4,3,1,0:T(8,128)} fusion(f32[2,16,64,8,32]{2,4,3,1,0:T(8,128)S(1)} %fusion.32, f32[2,16,64,9,32]{2,4,3,1,0:T(8,128)S(1)} %bitcast.163, f32[2,64,32]{1,2,0:T(8,128)S(1)} %copy.62), kind=kOutput, calls=%fused_computation.32 | convolution fusion | flops 201850880 | bytes 6569984 | tf_op jit(solution)/shard_map/v...bj,vji->v...bi/dot_general | solution.py:61
  137.5 3.4 %copy.65 = f32[2,16,64,256]{3,1,0,2:T(8,128)S(1)} copy(f32[2,16,64,256]{2,3,1,0:T(8,128)} %bitcast.181) | data formatting | bytes 4194304 | tf_op jit(solution)/shard_map/reshape | solution.py:67
  143.7 22.1 %reduce-scatter.3.cloned.1.call-done = f32[4,64,256]{2,1,0:T(8,128)} async-done(((f32[16,64,256]{2,1,0:T(8,128)}), f32[4,64,256]{2,1,0:T(8,128)}) %reduce-scatter.3.cloned.1.call-update) | async-done | bytes 262160 | tf_op jit(solution)/shard_map/reduce_scatter | solution.py:121
  165.8 1.7 multiply_multiply_fusion.1
  167.6 16.8 %all-gather.5.cloned.1.call-done = f32[16,64,256]{2,1,0:T(8,128)} async-done(((f32[4,64,256]{2,1,0:T(8,128)}), f32[16,64,256]{2,1,0:T(8,128)}) %all-gather.5.cloned.1.call-update) | async-done | bytes 1048592 | tf_op jit(solution)/shard_map/all_gather | solution.py:124
  185.5 3.4 %collective-permute-start.8 = (f32[16,16,256]{2,1,0:T(8,128)S(1)}, f32[16,16,256]{2,1,0:T(8,128)S(1)}, u32[]{:S(2)}, u32[]{:S(2)}) collective-permute-start(f32[16,16,256]{2,1,0:T(8,128)S(1)} %get-tuple-element.723), channel_id=1, source_target_pairs={{0,4},{1,5},{2,6},{3,7},{8,12},{9,13},{10,14},{11,15},{16,20},{17,... | collective-permute-start | bytes 786440 | tf_op jit(solution)/shard_map/ppermute | solution.py:18
  190.3 4.4 %collective-permute-done.8 = f32[16,16,256]{2,1,0:T(8,128)S(1)} collective-permute-done((f32[16,16,256]{2,1,0:T(8,128)S(1)}, f32[16,16,256]{2,1,0:T(8,128)S(1)}, u32[]{:S(2)}, u32[]{:S(2)}) %collective-permute-start.8) | collective-permute-done | bytes 262176 | tf_op jit(solution)/shard_map/ppermute | solution.py:18
  194.8 4.1 %collective-permute-done.9 = f32[16,16,256]{2,1,0:T(8,128)S(1)} collective-permute-done((f32[16,16,256]{2,1,0:T(8,128)S(1)}, f32[16,16,256]{2,1,0:T(8,128)S(1)}, u32[]{:S(2)}, u32[]{:S(2)}) %collective-permute-start.9) | collective-permute-done | bytes 262176 | tf_op jit(solution)/shard_map/ppermute | solution.py:19
  200.7 1.9 fusion.27
  202.7 2.1 convolution_add_fusion.4
  204.7 2.8 copy.67
  208.6 3.4 %collective-permute-start.10 = (f32[2,16,64,16]{2,3,1,0:T(8,128)S(1)}, f32[2,16,64,16]{2,3,1,0:T(8,128)S(1)}, u32[]{:S(2)}, u32[]{:S(2)}) collective-permute-start(f32[2,16,64,16]{2,3,1,0:T(8,128)S(1)} %get-tuple-element.709), channel_id=1, source_target_pairs={{0,1},{1,2},{2,3},{4,5},{5,6},{6,7},{8,9},{9,10},{10,11},{12,13},{... | collective-permute-start | bytes 393224 | tf_op jit(solution)/shard_map/ppermute | solution.py:18
  213.3 3.5 %collective-permute-done.10 = f32[2,16,64,16]{2,3,1,0:T(8,128)S(1)} collective-permute-done((f32[2,16,64,16]{2,3,1,0:T(8,128)S(1)}, f32[2,16,64,16]{2,3,1,0:T(8,128)S(1)}, u32[]{:S(2)}, u32[]{:S(2)}) %collective-permute-start.10) | collective-permute-done | bytes 131104 | tf_op jit(solution)/shard_map/ppermute | solution.py:18
  216.8 4.1 %collective-permute-done.11 = f32[2,16,64,16]{2,3,1,0:T(8,128)S(1)} collective-permute-done((f32[2,16,64,16]{2,3,1,0:T(8,128)S(1)}, f32[2,16,64,16]{2,3,1,0:T(8,128)S(1)}, u32[]{:S(2)}, u32[]{:S(2)}) %collective-permute-start.11) | collective-permute-done | bytes 131104 | tf_op jit(solution)/shard_map/ppermute | solution.py:19
  220.9 2.8 pad_maximum_fusion.2
  223.7 3.7 %fusion.29 = f32[2,16,64,8,32]{2,4,3,1,0:T(8,128)S(1)} fusion(f32[2,16,64,9,32]{2,4,3,1,0:T(8,128)S(1)} %bitcast.156, f32[2,64,32]{1,2,0:T(8,128)S(1)} %copy.51), kind=kOutput, calls=%fused_computation.68 | convolution fusion | flops 201326592 | bytes 4472832 | tf_op jit(solution)/shard_map/v...bj,vji->v...bi/dot_general | solution.py:64
  227.4 5.1 %convolution_add_fusion.1 = f32[2,16,64,8,32]{2,4,3,1,0:T(8,128)} fusion(f32[2,16,64,8,32]{2,4,3,1,0:T(8,128)S(1)} %fusion.29, f32[2,16,64,9,32]{2,4,3,1,0:T(8,128)S(1)} %bitcast.157, f32[2,64,32]{1,2,0:T(8,128)S(1)} %copy.51), kind=kOutput, calls=%fused_computation.31 | convolution fusion | flops 201850880 | bytes 6569984 | tf_op jit(solution)/shard_map/v...bj,vji->v...bi/dot_general | solution.py:61
  232.5 3.4 %copy.69 = f32[2,16,64,256]{3,1,2,0:T(8,128)S(1)} copy(f32[2,16,64,256]{2,3,1,0:T(8,128)} %bitcast.178) | data formatting | bytes 4194304 | tf_op jit(solution)/shard_map/reshape | solution.py:67
  235.9 3.9 %divide_select_fusion = f32[2,16,64,256]{3,1,2,0:T(8,128)S(1)} fusion(f32[2,16,64,256]{3,1,2,0:T(8,128)S(1)} %copy.69, f32[2,64,256]{2,1,0:T(8,128)S(1)} %bitcast.187, pred[2,64,256]{2,1,0:T(8,128)(4,1)S(1)} %bitcast.189, bf16[2,16,64,256]{3,2,1,0:T(8,128)(2,1)} %param.19, f32[2,16,16]{2,1,0:T(8,128)S(1)} %get-tuple-element.480), kind=kOutput, calls=%fused_computation.42 | convolution fusion | flops 102760448 | bytes 5408768 | tf_op jit(solution)/shard_map/vjyz,vji->viyz/dot_general | solution.py:72
  242.9 7.9 %collective-permute-done.12 = f32[2,16,16,256]{3,1,2,0:T(8,128)S(1)} collective-permute-done((f32[2,16,16,256]{3,1,2,0:T(8,128)S(1)}, f32[2,16,16,256]{3,1,2,0:T(8,128)S(1)}, u32[]{:S(2)}, u32[]{:S(2)}) %collective-permute-start.12) | collective-permute-done | bytes 524320 | tf_op jit(solution)/shard_map/ppermute | solution.py:18
  250.7 4.1 %collective-permute-done.13 = f32[2,16,16,256]{3,1,2,0:T(8,128)S(1)} collective-permute-done((f32[2,16,16,256]{3,1,2,0:T(8,128)S(1)}, f32[2,16,16,256]{3,1,2,0:T(8,128)S(1)}, u32[]{:S(2)}, u32[]{:S(2)}) %collective-permute-start.13) | collective-permute-done | bytes 524320 | tf_op jit(solution)/shard_map/ppermute | solution.py:19
  255.7 3.2 fusion.12
  259.0 3.4 %fusion.23 = f32[2,16,256,2,32]{2,4,3,1,0:T(8,128)S(1)} fusion(f32[2,16,256,2,32]{2,4,3,1,0:T(8,128)S(1)} %fusion.12, f32[2,16,256,2,32]{2,1,4,3,0:T(8,128)S(1)} %get-tuple-element.715, f32[2,64,32]{1,2,0:T(8,128)S(1)} %copy.57), kind=kOutput, calls=%fused_computation.46 | convolution fusion | flops 201850880 | bytes 6307840 | tf_op jit(solution)/shard_map/v...bj,vji->v...bi/dot_general | solution.py:61
  262.4 2.8 copy.72
  266.3 3.4 %collective-permute-start.14 = (f32[2,16,64,16]{2,3,1,0:T(8,128)S(1)}, f32[2,16,64,16]{2,3,1,0:T(8,128)S(1)}, u32[]{:S(2)}, u32[]{:S(2)}) collective-permute-start(f32[2,16,64,16]{2,3,1,0:T(8,128)S(1)} %get-tuple-element.707), channel_id=1, source_target_pairs={{0,1},{1,2},{2,3},{4,5},{5,6},{6,7},{8,9},{9,10},{10,11},{12,13},{... | collective-permute-start | bytes 393224 | tf_op jit(solution)/shard_map/ppermute | solution.py:18
  271.2 2.3 collective-permute-done.14
  273.5 4.4 %collective-permute-done.15 = f32[2,16,64,16]{2,3,1,0:T(8,128)S(1)} collective-permute-done((f32[2,16,64,16]{2,3,1,0:T(8,128)S(1)}, f32[2,16,64,16]{2,3,1,0:T(8,128)S(1)}, u32[]{:S(2)}, u32[]{:S(2)}) %collective-permute-start.15) | collective-permute-done | bytes 131104 | tf_op jit(solution)/shard_map/ppermute | solution.py:19
  277.9 2.8 pad_maximum_fusion.3
  280.7 3.7 %fusion.31 = f32[2,16,64,8,32]{2,4,3,1,0:T(8,128)S(1)} fusion(f32[2,16,64,9,32]{2,4,3,1,0:T(8,128)S(1)} %bitcast.158, f32[2,64,32]{1,2,0:T(8,128)S(1)} %copy.62), kind=kOutput, calls=%fused_computation.70 | convolution fusion | flops 201326592 | bytes 4472832 | tf_op jit(solution)/shard_map/v...bj,vji->v...bi/dot_general | solution.py:64
  284.4 5.1 %convolution_add_fusion = f32[2,16,64,8,32]{2,4,3,1,0:T(8,128)} fusion(f32[2,16,64,8,32]{2,4,3,1,0:T(8,128)S(1)} %fusion.31, f32[2,16,64,9,32]{2,4,3,1,0:T(8,128)S(1)} %bitcast.159, f32[2,64,32]{1,2,0:T(8,128)S(1)} %copy.62), kind=kOutput, calls=%fused_computation.30 | convolution fusion | flops 201850880 | bytes 6569984 | tf_op jit(solution)/shard_map/v...bj,vji->v...bi/dot_general | solution.py:61
  289.6 3.4 %copy.74 = f32[2,16,64,256]{3,1,0,2:T(8,128)S(1)} copy(f32[2,16,64,256]{2,3,1,0:T(8,128)} %bitcast.179) | data formatting | bytes 4194304 | tf_op jit(solution)/shard_map/reshape | solution.py:67
  295.8 22.2 %reduce-scatter.5.cloned.1.call-done = f32[4,64,256]{2,1,0:T(8,128)} async-done(((f32[16,64,256]{2,1,0:T(8,128)}), f32[4,64,256]{2,1,0:T(8,128)}) %reduce-scatter.5.cloned.1.call-update) | async-done | bytes 262160 | tf_op jit(solution)/shard_map/reduce_scatter | solution.py:121
  317.9 1.7 multiply_multiply_fusion
  (672 shorter events, 55.7 us)
Async XLA Ops:
  6.5 28.0 %copy-start = (f32[2,2,4]{2,1,0:T(2,128)S(1)}, f32[2,2,4]{2,1,0:T(2,128)}, u32[]{:S(2)}) copy-start(f32[2,2,4]{2,1,0:T(2,128)} %param.20) | copy-start | bytes 196
  6.5 21.8 %all-gather.3.cloned.1.call-start = ((), (), s32[]{:S(2)}) async-start(), calls=%async_computation.2 | async-start | bytes 1310720 | tf_op jit(solution)/shard_map/all_gather | solution.py:114
  7.3 158.6 %reduce-scatter.3.cloned.1.call-start = ((), (), s32[]{:S(2)}) async-start(), calls=%async_computation.3 | async-start | bytes 1310720 | tf_op jit(solution)/shard_map/reduce_scatter | solution.py:121
  29.4 9.4 %collective-permute-start = (f32[16,16,256]{2,1,0:T(8,128)S(1)}, f32[16,16,256]{2,1,0:T(8,128)S(1)}, u32[]{:S(2)}, u32[]{:S(2)}) collective-permute-start(f32[16,16,256]{2,1,0:T(8,128)S(1)} %get-tuple-element.725), channel_id=1, source_target_pairs={{0,4},{1,5},{2,6},{3,7},{8,12},{9,13},{10,14},{11,15},{16,20},{17,... | collective-permute-start | bytes 786440 | tf_op jit(solution)/shard_map/ppermute | solution.py:18
  32.9 10.0 %collective-permute-start.1 = (f32[16,16,256]{2,1,0:T(8,128)S(1)}, f32[16,16,256]{2,1,0:T(8,128)S(1)}, u32[]{:S(2)}, u32[]{:S(2)}) collective-permute-start(f32[16,16,256]{2,1,0:T(8,128)S(1)} %get-tuple-element.726), channel_id=1, source_target_pairs={{4,0},{5,1},{6,2},{7,3},{12,8},{13,9},{14,10},{15,11},{20,16},{21,... | collective-permute-start | bytes 786440 | tf_op jit(solution)/shard_map/ppermute | solution.py:19
  48.7 8.8 %copy-start.4 = (s32[2,2,4]{2,1,0:T(2,128)S(1)}, s32[2,2,4]{2,1,0:T(2,128)}, u32[]{:S(2)}) copy-start(s32[2,2,4]{2,1,0:T(2,128)} %param.21) | copy-start | bytes 196
  52.6 8.2 %collective-permute-start.2 = (f32[2,16,64,16]{2,3,1,0:T(8,128)S(1)}, f32[2,16,64,16]{2,3,1,0:T(8,128)S(1)}, u32[]{:S(2)}, u32[]{:S(2)}) collective-permute-start(f32[2,16,64,16]{2,3,1,0:T(8,128)S(1)} %get-tuple-element.713), channel_id=1, source_target_pairs={{0,1},{1,2},{2,3},{4,5},{5,6},{6,7},{8,9},{9,10},{10,11},{12,13},{... | collective-permute-start | bytes 393224 | tf_op jit(solution)/shard_map/ppermute | solution.py:18
  56.0 8.9 %collective-permute-start.3 = (f32[2,16,64,16]{2,3,1,0:T(8,128)S(1)}, f32[2,16,64,16]{2,3,1,0:T(8,128)S(1)}, u32[]{:S(2)}, u32[]{:S(2)}) collective-permute-start(f32[2,16,64,16]{2,3,1,0:T(8,128)S(1)} %get-tuple-element.714), channel_id=1, source_target_pairs={{1,0},{2,1},{3,2},{5,4},{6,5},{7,6},{9,8},{10,9},{11,10},{13,12},{... | collective-permute-start | bytes 393224 | tf_op jit(solution)/shard_map/ppermute | solution.py:19
  86.3 11.2 %collective-permute-start.4 = (f32[2,16,16,256]{3,1,2,0:T(8,128)}, f32[2,16,16,256]{3,1,2,0:T(8,128)S(1)}, u32[]{:S(2)}, u32[]{:S(2)}) collective-permute-start(f32[2,16,16,256]{3,1,2,0:T(8,128)} %get-tuple-element.721), channel_id=1, source_target_pairs={{0,4},{1,5},{2,6},{3,7},{8,12},{9,13},{10,14},{11,15},{16,20},{17,... | collective-permute-start | bytes 1572872 | tf_op jit(solution)/shard_map/ppermute | solution.py:18
  87.8 13.8 %collective-permute-start.5 = (f32[2,16,16,256]{3,1,2,0:T(8,128)}, f32[2,16,16,256]{3,1,2,0:T(8,128)}, u32[]{:S(2)}, u32[]{:S(2)}) collective-permute-start(f32[2,16,16,256]{3,1,2,0:T(8,128)} %get-tuple-element.722), channel_id=1, source_target_pairs={{4,0},{5,1},{6,2},{7,3},{12,8},{13,9},{14,10},{15,11},{20,16},{21,... | collective-permute-start | bytes 1572872 | tf_op jit(solution)/shard_map/ppermute | solution.py:19
  114.2 8.3 %collective-permute-start.6 = (f32[2,16,64,16]{2,3,1,0:T(8,128)S(1)}, f32[2,16,64,16]{2,3,1,0:T(8,128)S(1)}, u32[]{:S(2)}, u32[]{:S(2)}) collective-permute-start(f32[2,16,64,16]{2,3,1,0:T(8,128)S(1)} %get-tuple-element.711), channel_id=1, source_target_pairs={{0,1},{1,2},{2,3},{4,5},{5,6},{6,7},{8,9},{9,10},{10,11},{12,13},{... | collective-permute-start | bytes 393224 | tf_op jit(solution)/shard_map/ppermute | solution.py:18
  117.6 8.3 %collective-permute-start.7 = (f32[2,16,64,16]{2,3,1,0:T(8,128)S(1)}, f32[2,16,64,16]{2,3,1,0:T(8,128)S(1)}, u32[]{:S(2)}, u32[]{:S(2)}) collective-permute-start(f32[2,16,64,16]{2,3,1,0:T(8,128)S(1)} %get-tuple-element.712), channel_id=1, source_target_pairs={{1,0},{2,1},{3,2},{5,4},{6,5},{7,6},{9,8},{10,9},{11,10},{13,12},{... | collective-permute-start | bytes 393224 | tf_op jit(solution)/shard_map/ppermute | solution.py:19
  140.9 25.0 %copy-start.3 = (f32[4,64,256]{2,1,0:T(8,128)S(1)}, f32[4,64,256]{2,1,0:T(8,128)}, u32[]{:S(2)}) copy-start(f32[4,64,256]{2,1,0:T(8,128)} %param.18) | copy-start | bytes 786436
  143.6 40.8 %all-gather.5.cloned.1.call-start = ((), (), s32[]{:S(2)}) async-start(), calls=%async_computation.4 | async-start | bytes 1310720 | tf_op jit(solution)/shard_map/all_gather | solution.py:124
  167.5 150.4 %reduce-scatter.5.cloned.1.call-start = ((), (), s32[]{:S(2)}) async-start(), calls=%async_computation.5 | async-start | bytes 1310720 | tf_op jit(solution)/shard_map/reduce_scatter | solution.py:121
  185.5 9.3 %collective-permute-start.8 = (f32[16,16,256]{2,1,0:T(8,128)S(1)}, f32[16,16,256]{2,1,0:T(8,128)S(1)}, u32[]{:S(2)}, u32[]{:S(2)}) collective-permute-start(f32[16,16,256]{2,1,0:T(8,128)S(1)} %get-tuple-element.723), channel_id=1, source_target_pairs={{0,4},{1,5},{2,6},{3,7},{8,12},{9,13},{10,14},{11,15},{16,20},{17,... | collective-permute-start | bytes 786440 | tf_op jit(solution)/shard_map/ppermute | solution.py:18
  188.9 10.0 %collective-permute-start.9 = (f32[16,16,256]{2,1,0:T(8,128)S(1)}, f32[16,16,256]{2,1,0:T(8,128)S(1)}, u32[]{:S(2)}, u32[]{:S(2)}) collective-permute-start(f32[16,16,256]{2,1,0:T(8,128)S(1)} %get-tuple-element.724), channel_id=1, source_target_pairs={{4,0},{5,1},{6,2},{7,3},{12,8},{13,9},{14,10},{15,11},{20,16},{21,... | collective-permute-start | bytes 786440 | tf_op jit(solution)/shard_map/ppermute | solution.py:19
  208.6 8.2 %collective-permute-start.10 = (f32[2,16,64,16]{2,3,1,0:T(8,128)S(1)}, f32[2,16,64,16]{2,3,1,0:T(8,128)S(1)}, u32[]{:S(2)}, u32[]{:S(2)}) collective-permute-start(f32[2,16,64,16]{2,3,1,0:T(8,128)S(1)} %get-tuple-element.709), channel_id=1, source_target_pairs={{0,1},{1,2},{2,3},{4,5},{5,6},{6,7},{8,9},{9,10},{10,11},{12,13},{... | collective-permute-start | bytes 393224 | tf_op jit(solution)/shard_map/ppermute | solution.py:18
  212.0 8.9 %collective-permute-start.11 = (f32[2,16,64,16]{2,3,1,0:T(8,128)S(1)}, f32[2,16,64,16]{2,3,1,0:T(8,128)S(1)}, u32[]{:S(2)}, u32[]{:S(2)}) collective-permute-start(f32[2,16,64,16]{2,3,1,0:T(8,128)S(1)} %get-tuple-element.710), channel_id=1, source_target_pairs={{1,0},{2,1},{3,2},{5,4},{6,5},{7,6},{9,8},{10,9},{11,10},{13,12},{... | collective-permute-start | bytes 393224 | tf_op jit(solution)/shard_map/ppermute | solution.py:19
  239.9 10.9 %collective-permute-start.12 = (f32[2,16,16,256]{3,1,2,0:T(8,128)S(1)}, f32[2,16,16,256]{3,1,2,0:T(8,128)S(1)}, u32[]{:S(2)}, u32[]{:S(2)}) collective-permute-start(f32[2,16,16,256]{3,1,2,0:T(8,128)S(1)} %get-tuple-element.719), channel_id=1, source_target_pairs={{0,4},{1,5},{2,6},{3,7},{8,12},{9,13},{10,14},{11,15},{16,20},{17,... | collective-permute-start | bytes 1572872 | tf_op jit(solution)/shard_map/ppermute | solution.py:18
  241.3 13.5 %collective-permute-start.13 = (f32[2,16,16,256]{3,1,2,0:T(8,128)S(1)}, f32[2,16,16,256]{3,1,2,0:T(8,128)S(1)}, u32[]{:S(2)}, u32[]{:S(2)}) collective-permute-start(f32[2,16,16,256]{3,1,2,0:T(8,128)S(1)} %get-tuple-element.720), channel_id=1, source_target_pairs={{4,0},{5,1},{6,2},{7,3},{12,8},{13,9},{14,10},{15,11},{20,16},{21,... | collective-permute-start | bytes 1572872 | tf_op jit(solution)/shard_map/ppermute | solution.py:19
  266.3 7.3 %collective-permute-start.14 = (f32[2,16,64,16]{2,3,1,0:T(8,128)S(1)}, f32[2,16,64,16]{2,3,1,0:T(8,128)S(1)}, u32[]{:S(2)}, u32[]{:S(2)}) collective-permute-start(f32[2,16,64,16]{2,3,1,0:T(8,128)S(1)} %get-tuple-element.707), channel_id=1, source_target_pairs={{0,1},{1,2},{2,3},{4,5},{5,6},{6,7},{8,9},{9,10},{10,11},{12,13},{... | collective-permute-start | bytes 393224 | tf_op jit(solution)/shard_map/ppermute | solution.py:18
  269.7 8.3 %collective-permute-start.15 = (f32[2,16,64,16]{2,3,1,0:T(8,128)S(1)}, f32[2,16,64,16]{2,3,1,0:T(8,128)S(1)}, u32[]{:S(2)}, u32[]{:S(2)}) collective-permute-start(f32[2,16,64,16]{2,3,1,0:T(8,128)S(1)} %get-tuple-element.708), channel_id=1, source_target_pairs={{1,0},{2,1},{3,2},{5,4},{6,5},{7,6},{9,8},{10,9},{11,10},{13,12},{... | collective-permute-start | bytes 393224 | tf_op jit(solution)/shard_map/ppermute | solution.py:19
  289.6 30.1 %copy-start.1 = (f32[2,2,4]{2,1,0:T(2,128)S(1)}, f32[2,2,4]{2,1,0:T(2,128)}, u32[]{:S(2)}) copy-start(f32[2,2,4]{2,1,0:T(2,128)} %param.20) | copy-start | bytes 196
  293.0 25.0 %copy-start.2 = (f32[4,64,256]{2,1,0:T(8,128)S(1)}, f32[4,64,256]{2,1,0:T(8,128)}, u32[]{:S(2)}) copy-start(f32[4,64,256]{2,1,0:T(8,128)} %multiply_multiply_fusion.1) | copy-start | bytes 786436
Sparse Core Ops, SparseCore 0:
  8.9 19.4 all-gather.2
  143.8 22.0 reduce-scatter.2
  167.7 16.6 all-gather.4
  295.9 22.0 reduce-scatter.4
where the time goes:
time: 332 us; the launch traced here: 327 us
  waiting for transfers between devices  129 us (39%)
  matrix products  67.7 us (20%)
  local copies, waits for them, and re-layouts  41.3 us (12%)
  other arithmetic  37.7 us (11%)
  starting transfers between devices  35.4 us (11%)
  between operations  14.1 us (4%)
    reduce_scatter x2, waiting for transfers between devices, per_device(): lax.psum_scatter(summed, 'view', scatter_dimension=0, tiled=True)  44.3 us
    ppermute x8, waiting for transfers between devices, extended(): after = lax.ppermute(first, axis, down)  32.6 us
    dot_general x8, matrix products, axis_blur(): jnp.einsum('v...bj,vji->v...bi', tiles[..., :-1, :], bands[:, :width], pr...  31.6 us
    ppermute x8, waiting for transfers between devices, extended(): before = lax.ppermute(last, axis, up)  29.7 us
    reshape x8, local copies, waits for them, and re-layouts, axis_blur(): joined = (early + later).reshape(moved.shape[:-1] + (count * width,))  25.4 us
    dot_general x8, matrix products, axis_blur(): jnp.einsum('v...bj,vji->v...bi', tiles[..., 1:, :], bands[:, width:], pre...  25.2 us
    ppermute x8, starting transfers between devices, extended(): before = lax.ppermute(last, axis, up)  23.3 us
    all_gather x1, waiting for transfers between devices, per_device(): current = lax.all_gather(owned_planes, 'view', axis=0, tiled=True)  16.8 us
  transfers between devices with their start and end apart: 20, of which 19 were waited for; matrix products, arithmetic and copies ran while one was open for 7% of the time, Pallas kernels for 0%

commit v1 on v0

v1 whole, which is shorter than its diff:
```python
import functools

import jax
import jax.numpy as jnp
from jax import lax
from jax.experimental import pallas as pl
from jax.experimental.pallas import tpu as pltpu
from jax.sharding import PartitionSpec as P

BY = 32
BZ = 64
ITERS = 2
LANES = 128
MESH = pl.DeviceIdType.MESH
BF = jnp.bfloat16
F32 = jnp.float32


def kernel_table(profile, supports):
    tap_count = profile.shape[-1]
    distance = jnp.abs(jnp.arange(tap_count, dtype=jnp.int32) - (tap_count - 1) // 2)
    inside = distance[None, None, :] <= supports[:, :, None]
    masked = jnp.where(inside, profile, 0.0)
    return masked / jnp.sum(masked, axis=-1, keepdims=True)


def lane_iota(rows):
    return lax.broadcasted_iota(jnp.int32, (rows, LANES), 1)


def toeplitz(row, rows, shift):
    wide = jnp.broadcast_to(row, (rows, LANES))
    return pltpu.roll(wide, shift % LANES, 1, stride=1, stride_axis=0)


def roll_lanes(x, shift):
    shift = shift % LANES
    return pltpu.roll(x, shift, 1) if shift else x


def build_plane_row(dst, row_base, kx, ky, planes, hw):
    lane = lane_iota(hw)
    per_tile = LANES // hw
    halves = planes // per_tile
    tall = toeplitz(ky, hw, 0)
    bands = []
    for d in range(3):
        q = jnp.where(lane < hw, roll_lanes(tall, -hw * d), 0.0)
        width = hw
        while width < LANES:
            q = q + roll_lanes(q, width)
            width *= 2
        bands.append(q)
    tx = toeplitz(kx, planes, -hw)
    row_id = lax.broadcasted_iota(jnp.int32, (LANES, LANES), 0)
    group = lax.broadcasted_iota(jnp.int32, (LANES, LANES), 1) // hw
    for half in range(halves):
        pick = (row_id == group + half * per_tile).astype(F32)
        spread = jnp.dot(tx, pick, precision=lax.Precision.HIGHEST, preferred_element_type=F32)
        for d in range(3):
            for x in range(planes):
                tile = spread[x : x + 1, :] * bands[d]
                c0 = (halves * d + half) * LANES
                dst[row_base + x * hw : row_base + (x + 1) * hw, c0 : c0 + LANES] = tile.astype(BF)


def build_depth(dst, v, kz, rows_z, hw):
    row_j = lax.broadcasted_iota(jnp.int32, (rows_z, LANES), 0)
    lane = lane_iota(rows_z)
    reps = rows_z // LANES
    t = jnp.concatenate([toeplitz(kz, LANES, -hw)] * reps, axis=0)
    for ct in range(reps):
        c = lane + ct * LANES
        keep = jnp.abs(c - row_j) <= hw
        dst[v, :, ct * LANES : (ct + 1) * LANES] = jnp.where(keep, t, 0.0).astype(BF)
    h = jnp.concatenate([toeplitz(kz, LANES, 0)] * reps, axis=0)
    low = (row_j < hw) & (lane < hw)
    high = (row_j >= rows_z - hw) & (lane >= hw) & (lane < 2 * hw)
    h = jnp.where(low | high, h, 0.0)
    width = 2 * hw
    while width < LANES:
        h = h + roll_lanes(h, width)
        width *= 2
    dst[v, :, rows_z : rows_z + LANES] = h.astype(BF)


def kernel(
    sizes, est, vd, scales, flags, taps, out,
    fg, pk, wk, wl, wr, fb, am, bm, mt, gp, ob, zp,
    r1, r1z, s2, s2z, r2, r2z, ub, zu, zl, zr, yu, yd, ssem, rsem,
):
    ny, nz, views, planes, rows_y, rows_z, own, hw = sizes
    nb = rows_y // hw
    ne = nb + 2
    blk = planes * hw
    v = lax.axis_index("view")
    gy = lax.axis_index("gy")
    gz = lax.axis_index("gz")
    va, vb, vc = (lax.bitwise_xor(v, 1), lax.bitwise_xor(v, 2), lax.bitwise_xor(v, 3))
    has_up, has_dn = (gy > 0, gy < ny - 1)
    has_lf, has_rt = (gz > 0, gz < nz - 1)
    to_a, to_b = ({"view": va}, {"view": vb})
    to_up, to_dn = ({"gy": jnp.maximum(gy - 1, 0)}, {"gy": jnp.minimum(gy + 1, ny - 1)})
    to_lf, to_rt = ({"gz": jnp.maximum(gz - 1, 0)}, {"gz": jnp.minimum(gz + 1, nz - 1)})
    view_total = views * 4

    def mine(o):
        return pl.ds(o * own, own)

    def rcopy(src, dst, it, sid, dev):
        return pltpu.make_async_remote_copy(
            src_ref=src, dst_ref=dst, send_sem=ssem.at[it, sid], recv_sem=rsem.at[it, sid],
            device_id=dev, device_id_type=MESH,
        )

    def landed(dst, it, sid, dev):
        rcopy(dst, dst, it, sid, dev).wait_recv()

    def sent(src, it, sid, dev):
        rcopy(src, src, it, sid, dev).wait_send()

    for ref in (wl, wr, zl, zr, yu, yd, zp):
        ref[...] = jnp.zeros_like(ref)
    for e in (0, nb + 1):
        fg[e] = jnp.zeros((planes, hw, rows_z), F32)
    for vv in range(views):
        for e in (0, 1, nb + 2, nb + 3):
            gp[vv, e * blk : (e + 1) * blk, :] = jnp.zeros((blk, rows_z + LANES), BF)
    for b in range(nb):
        for p in range(own):
            fg[1 + b, own * v + p] = est[p, b * hw : (b + 1) * hw, :]

    barrier = pltpu.get_barrier_semaphore()
    for dev in (to_a, to_b):
        pl.semaphore_signal(barrier, inc=1, device_id=dev, device_id_type=MESH)
    for cond, dev in ((has_up, to_up), (has_dn, to_dn), (has_lf, to_lf), (has_rt, to_rt)):
        @pl.when(cond)
        def _():
            pl.semaphore_signal(barrier, inc=1, device_id=dev, device_id_type=MESH)
    sides = [c.astype(jnp.int32) for c in (has_up, has_dn, has_lf, has_rt)]
    pl.semaphore_wait(barrier, 2 + sides[0] + sides[1] + sides[2] + sides[3])

    s_p = 3 * ne
    s_yu, s_yd, s_zl, s_zr = (3 * ne + 3, 3 * ne + 4, 3 * ne + 5, 3 * ne + 6)
    s_r1 = 3 * ne + 7
    s_r2 = s_r1 + 2 * ne
    s_z = s_r2 + ne
    s_rl, s_rr, s_ru, s_rd = (s_z + 3, s_z + 4, s_z + 5, s_z + 6)

    def when_edge(e, fn):
        if e == 0:
            pl.when(has_up)(fn)
        elif e == nb + 1:
            pl.when(has_dn)(fn)
        else:
            fn()

    lane_h = lane_iota(hw)
    group_h = lane_h // (2 * hw)
    side_h = (lane_h // hw) % 2

    for it in range(ITERS):
        own_sl = mine(v)

        def ag_start(e):
            rcopy(fg.at[e, own_sl], fg.at[e, own_sl], it, ne + e, to_b).start()
            rcopy(fg.at[e, own_sl], fg.at[e, own_sl], it, e, to_a).start()

        def ag_forward(e):
            landed(fg.at[e, mine(vb)], it, ne + e, to_b)
            rcopy(fg.at[e, mine(vb)], fg.at[e, mine(vb)], it, 2 * ne + e, to_a).start()

        @pl.when(has_dn)
        def _():
            rcopy(fg.at[nb, own_sl], fg.at[0, own_sl], it, s_yd, to_dn).start()

        @pl.when(has_up)
        def _():
            rcopy(fg.at[1, own_sl], fg.at[nb + 1, own_sl], it, s_yu, to_up).start()

        for b in range(nb):
            ag_start(1 + b)

        if it == 0:
            for vv in range(views):
                build_depth(mt, vv, taps[0, 3 * vv + 2 : 3 * vv + 3, :], rows_z, hw)
                build_plane_row(
                    am, vv * blk, taps[0, 3 * vv : 3 * vv + 1, :],
                    taps[0, 3 * vv + 1 : 3 * vv + 2, :], planes, hw,
                )

        @pl.when(has_up)
        def _():
            landed(fg.at[0, own_sl], it, s_yd, to_up)
            ag_start(0)

        @pl.when(has_dn)
        def _():
            landed(fg.at[nb + 1, own_sl], it, s_yu, to_dn)
            ag_start(nb + 1)

        for e in range(ne):
            packed = jnp.zeros((hw, LANES), F32)
            for p in range(own):
                body = fg[e, own * v + p]
                first = roll_lanes(body[:, :LANES], 2 * hw * p + hw)
                last = roll_lanes(body[:, rows_z - LANES :], 2 * hw * p + hw)
                pair = jnp.where(side_h == 0, last, first)
                packed = jnp.where(group_h == p, pair, packed)
            wk[e] = packed

        @pl.when(has_lf)
        def _():
            rcopy(wk, wr, it, s_zl, to_lf).start()

        @pl.when(has_rt)
        def _():
            rcopy(wk, wl, it, s_zr, to_rt).start()

        ag_forward(1)

        if it == 0:
            for vv in range(views):
                build_plane_row(
                    bm.at[vv], 0, taps[1, 3 * vv : 3 * vv + 1, :],
                    taps[1, 3 * vv + 1 : 3 * vv + 2, :], planes, hw,
                )

        @pl.when(has_lf)
        def _():
            landed(wl, it, s_zr, to_lf)

        @pl.when(has_rt)
        def _():
            landed(wr, it, s_zl, to_rt)

        for e in range(ne):
            pk[v, e] = jnp.where(side_h == 0, wl[e], wr[e])
        rcopy(pk.at[v], pk.at[v], it, s_p + 1, to_b).start()
        rcopy(pk.at[v], pk.at[v], it, s_p, to_a).start()

        for b in range(1, nb):
            ag_forward(1 + b)
        for e in (0, nb + 1):
            when_edge(e, functools.partial(ag_forward, e))
        landed(pk.at[vb], it, s_p + 1, to_b)
        rcopy(pk.at[vb], pk.at[vb], it, s_p + 2, to_a).start()

        for e in range(ne):
            def arrivals(e=e):
                landed(fg.at[e, mine(va)], it, e, to_a)
                landed(fg.at[e, mine(vc)], it, 2 * ne + e, to_a)
            when_edge(e, arrivals)
        landed(pk.at[va], it, s_p, to_a)
        landed(pk.at[vc], it, s_p + 2, to_a)

        @pl.loop(0, ne)
        def _(e):
            base = pl.multiple_of(e * blk, blk)
            fb[pl.ds(base, blk), :rows_z] = fg[e].reshape(blk, rows_z).astype(BF)
            for x in range(planes):
                rim = jnp.where(group_h == x % own, pk[x // own, e], 0.0)
                fb[pl.ds(base + x * hw, hw), rows_z:] = rim.astype(BF)

        @pl.loop(0, nb)
        def _(b):
            base = pl.multiple_of(b * blk, blk)
            g = jnp.dot(am[...], fb[pl.ds(base, 3 * blk), :], preferred_element_type=F32).astype(BF)
            z_block = lax.broadcasted_iota(jnp.int32, (1, rows_z), 1) // BZ
            y_block = b * hw // BY
            for vv in range(views):
                scale = jnp.zeros((1, rows_z), F32)
                valid = jnp.zeros((1, rows_z), jnp.int32)
                for c in range(rows_z // BZ):
                    scale = jnp.where(z_block == c, scales[vv, y_block, c], scale)
                    valid = jnp.where(z_block == c, flags[vv, y_block, c], valid)
                blurred = lax.dot_general(
                    g[vv * blk : (vv + 1) * blk], mt[vv], (((1,), (1,)), ((), ())),
                    preferred_element_type=F32,
                )
                data = vd[vv, :, pl.ds(pl.multiple_of(b * hw, hw), hw), :].astype(F32)
                ratio = jnp.where(valid == 1, data.reshape(blk, rows_z) * scale / blurred, 1.0)
                spread = jnp.dot(ratio.astype(BF), mt[vv], preferred_element_type=F32)
                gp[vv, pl.ds(base + 2 * blk, blk), :] = spread.astype(BF)

        @pl.when(has_dn)
        def _():
            sent(fg.at[nb, own_sl], it, s_yd, to_dn)

        @pl.when(has_up)
        def _():
            sent(fg.at[1, own_sl], it, s_yu, to_up)

        @pl.when(has_lf)
        def _():
            sent(wk, it, s_zl, to_lf)

        @pl.when(has_rt)
        def _():
            sent(wk, it, s_zr, to_rt)

        for e in range(ne):
            def sends(e=e):
                sent(fg.at[e, own_sl], it, e, to_a)
                sent(fg.at[e, own_sl], it, ne + e, to_b)
                sent(fg.at[e, mine(vb)], it, 2 * ne + e, to_a)
            when_edge(e, sends)
        sent(pk.at[v], it, s_p, to_a)
        sent(pk.at[v], it, s_p + 1, to_b)
        sent(pk.at[vb], it, s_p + 2, to_a)

        def used(e):
            return ((e > 0) | has_up) & ((e < nb + 1) | has_dn)

        def r1_copy(e, k):
            owner = (va, vc)[k]
            return rcopy(ob.at[e, mine(owner)], r1.at[e, k], it, s_r1 + 2 * e + k, to_a)

        @pl.loop(0, ne)
        def _(e):
            @pl.when(used(e))
            def _():
                rows = pl.ds(pl.multiple_of(e * blk, blk), 3 * blk)
                total = jnp.dot(bm[0], gp[0, rows, :], preferred_element_type=F32)
                for vv in range(1, views):
                    total = total + jnp.dot(bm[vv], gp[vv, rows, :], preferred_element_type=F32)
                ob[e] = total[:, :rows_z].reshape(planes, hw, rows_z)
                r1_copy(e, 1).start()
                r1_copy(e, 0).start()
                rims = total[:, rows_z:].reshape(planes, hw, LANES)
                for o in range(planes // own):
                    packed = rims[own * o]
                    for p in range(1, own):
                        packed = jnp.where(group_h == p, rims[own * o + p], packed)
                    zp[o, e] = packed

        rcopy(zp.at[vc], r1z.at[1], it, s_z + 1, to_a).start()
        rcopy(zp.at[va], r1z.at[0], it, s_z, to_a).start()

        @pl.loop(0, ne)
        def _(e):
            @pl.when(used(e))
            def _():
                r1_copy(e, 1).wait_recv()
                s2[e] = ob[e, mine(vb)] + r1[e, 1]
                rcopy(s2.at[e], r2.at[e], it, s_r2 + e, to_b).start()

        landed(r1z.at[1], it, s_z + 1, to_a)
        s2z[...] = zp[vb] + r1z[1]
        rcopy(s2z, r2z, it, s_z + 2, to_b).start()

        @pl.loop(0, ne)
        def _(e):
            @pl.when(used(e))
            def _():
                r1_copy(e, 0).wait_recv()
                landed(r2.at[e], it, s_r2 + e, to_b)
                ub[e] = ob[e, own_sl] + r1[e, 0] + r2[e]

        landed(r1z.at[0], it, s_z, to_a)
        landed(r2z, it, s_z + 2, to_b)
        zu[...] = zp[v] + r1z[0] + r2z[...]

        @pl.when(has_lf)
        def _():
            rcopy(zu, zr, it, s_rl, to_lf).start()

        @pl.when(has_rt)
        def _():
            rcopy(zu, zl, it, s_rr, to_rt).start()

        @pl.when(has_rt)
        def _():
            landed(zr, it, s_rl, to_rt)

        @pl.when(has_lf)
        def _():
            landed(zl, it, s_rr, to_lf)

        for e in range(ne):
            def add_rims(e=e):
                for p in range(own):
                    last = roll_lanes(zr[e], LANES - hw - 2 * hw * p)
                    first = roll_lanes(zl[e], -(2 * hw * p + hw))
                    ub[e, p, :, :LANES] += jnp.where(lane_h < hw, first, 0.0)
                    ub[e, p, :, rows_z - LANES :] += jnp.where(lane_h >= LANES - hw, last, 0.0)
            when_edge(e, add_rims)

        @pl.when(has_up)
        def _():
            rcopy(ub.at[0], yd, it, s_ru, to_up).start()

        @pl.when(has_dn)
        def _():
            rcopy(ub.at[nb + 1], yu, it, s_rd, to_dn).start()

        @pl.when(has_dn)
        def _():
            landed(yd, it, s_ru, to_dn)

        @pl.when(has_up)
        def _():
            landed(yu, it, s_rd, to_up)

        for b in range(nb):
            for p in range(own):
                total = ub[1 + b, p]
                if b == 0:
                    total = total + yu[p]
                if b == nb - 1:
                    total = total + yd[p]
                fresh = fg[1 + b, own * v + p] * total / view_total
                if it + 1 < ITERS:
                    fg[1 + b, own * v + p] = fresh
                else:
                    out[p, b * hw : (b + 1) * hw, :] = fresh

        @pl.loop(0, ne)
        def _(e):
            @pl.when(used(e))
            def _():
                r1_copy(e, 0).wait_send()
                r1_copy(e, 1).wait_send()
                sent(s2.at[e], it, s_r2 + e, to_b)

        sent(zp.at[va], it, s_z, to_a)
        sent(zp.at[vc], it, s_z + 1, to_a)
        sent(s2z, it, s_z + 2, to_b)

        @pl.when(has_lf)
        def _():
            sent(zu, it, s_rl, to_lf)

        @pl.when(has_rt)
        def _():
            sent(zu, it, s_rr, to_rt)

        @pl.when(has_up)
        def _():
            sent(ub.at[0], it, s_ru, to_up)

        @pl.when(has_dn)
        def _():
            sent(ub.at[nb + 1], it, s_rd, to_dn)


def per_device(ny, nz, estimate, view_data, block_scales, block_flags, profile, supports):
    views, planes, rows_y, rows_z = view_data.shape
    own = estimate.shape[0]
    hw = (profile.shape[2] - 1) // 2
    nb = rows_y // hw
    ne = nb + 2
    blk = planes * hw
    wide = rows_z + LANES
    forward = kernel_table(profile, supports)
    both = jnp.stack([forward, forward[:, :, ::-1]]).reshape(2, views * 3, profile.shape[2])
    taps = jnp.pad(both, ((0, 0), (0, 0), (0, LANES - profile.shape[2])))
    owners = planes // own
    n_sem = 6 * ne + 7 + 7
    vm = pltpu.VMEM
    scratch = [
        vm((ne, planes, hw, rows_z), F32),
        vm((owners, ne, hw, LANES), F32),
        vm((ne, hw, LANES), F32),
        vm((ne, hw, LANES), F32),
        vm((ne, hw, LANES), F32),
        vm((ne * blk, wide), BF),
        vm((views * blk, 3 * blk), BF),
        vm((views, blk, 3 * blk), BF),
        vm((views, rows_z, wide), BF),
        vm((views, (nb + 4) * blk, wide), BF),
        vm((ne, planes, hw, rows_z), F32),
        vm((owners, ne, hw, LANES), F32),
        vm((ne, 2, own, hw, rows_z), F32),
        vm((2, ne, hw, LANES), F32),
        vm((ne, own, hw, rows_z), F32),
        vm((ne, hw, LANES), F32),
        vm((ne, own, hw, rows_z), F32),
        vm((ne, hw, LANES), F32),
        vm((ne, own, hw, rows_z), F32),
        vm((ne, hw, LANES), F32),
        vm((ne, hw, LANES), F32),
        vm((ne, hw, LANES), F32),
        vm((own, hw, rows_z), F32),
        vm((own, hw, rows_z), F32),
        pltpu.SemaphoreType.DMA((ITERS, n_sem)),
        pltpu.SemaphoreType.DMA((ITERS, n_sem)),
    ]
    in_vm = pl.BlockSpec(memory_space=pltpu.VMEM)
    in_sm = pl.BlockSpec(memory_space=pltpu.SMEM)
    return pl.pallas_call(
        functools.partial(kernel, (ny, nz, views, planes, rows_y, rows_z, own, hw)),
        out_shape=jax.ShapeDtypeStruct(estimate.shape, F32),
        in_specs=[in_vm, in_vm, in_sm, in_sm, in_vm],
        out_specs=in_vm,
        scratch_shapes=scratch,
        compiler_params=pltpu.CompilerParams(collective_id=0, has_side_effects=True),
    )(estimate, view_data, block_scales, block_flags, taps)


def solution(mesh):
    placed = (
        P("view", "gy", "gz"),
        P("view", None, "gy", "gz"),
        P("view", "gy", "gz"),
        P("view", "gy", "gz"),
        P("view", None, None),
        P("view", None),
    )
    body = functools.partial(per_device, mesh.shape["gy"], mesh.shape["gz"])
    return jax.shard_map(
        body, mesh=mesh, in_specs=placed, out_specs=P("view", "gy", "gz"), check_vma=False
    )
```

time: 332 us -> 80.5 us (0.24); the launches traced: 327 us -> 80.3 us
  waiting for transfers between devices: 129 us -> 0 us
  Pallas kernels: 0 us -> 76.9 us
  matrix products: 67.7 us -> 0 us
  local copies, waits for them, and re-layouts: 41.3 us -> 2.57 us
  other arithmetic: 37.7 us -> 0.85 us
  starting transfers between devices: 35.4 us -> 0 us
  between operations: 14.1 us -> 0.02 us
    pallas_call x0 -> x1, Pallas kernels: none -> 76.9 us  [per_device(): pl.pallas_call(functools.partial(kernel, (ny, nz, views, planes, rows_y,...]
    dot_general x22 -> x0, matrix products: 67.7 us -> none  [the longest x8 31.6 us: axis_blur(): jnp.einsum('v...bj,vji->v...bi', tiles[..., :-1, :], bands[:, :width], pr...]
    ppermute x16 -> x0, waiting for transfers between devices: 62.3 us -> none  [the longest x8 32.6 us: extended(): after = lax.ppermute(first, axis, down)]
    reduce_scatter x2 -> x0, waiting for transfers between devices: 44.3 us -> none  [per_device(): lax.psum_scatter(summed, 'view', scatter_dimension=0, tiled=True)]
    ppermute x16 -> x0, starting transfers between devices: 35.3 us -> none  [the longest x8 23.3 us: extended(): before = lax.ppermute(last, axis, up)]
    reshape x8 -> x0, local copies, waits for them, and re-layouts: 25.4 us -> none  [axis_blur(): joined = (early + later).reshape(moved.shape[:-1] + (count * width,))]
    all_gather x2 -> x0, waiting for transfers between devices: 21.6 us -> none  [the longest x1 16.8 us: per_device(): current = lax.all_gather(owned_planes, 'view', axis=0, tiled=True)]
    concatenate x8 -> x0, other arithmetic: 15.6 us -> none  [extended(): x = jnp.concatenate([before, x, after], axis=dim)]
  transfers between devices with their start and end apart: 20 -> 0, of which waited for: 19 -> 0; matrix products, arithmetic and copies ran while one was open for 7% -> 0% of each run, Pallas kernels for 0% -> 0%
where the time goes in v1:
time: 80.5 us; the launch traced here: 80.3 us
  Pallas kernels  76.9 us (96%)
  local copies, waits for them, and re-layouts  2.57 us (3%)
  other arithmetic  0.85 us (1%)
    pallas_call x1, Pallas kernels, per_device(): pl.pallas_call(functools.partial(kernel, (ny, nz, views, planes, rows_y,...  76.9 us
    unnamed x4, local copies, waits for them, and re-layouts  2.45 us

profile of v1, /device:TPU:0, one launch (start us, length us, event | category | flops | bytes accessed | tf_op | source)
XLA Modules:
  0.0 80.3 jit_solution(16295955789809255646)
XLA Ops:
  0.0 0.0 copy-start
  0.0 0.8 copy.10
  0.8 0.0 copy-done
  0.8 0.2 fusion.1
  0.9 0.1 fusion
  1.0 0.1 rev.3
  1.1 0.6 select_maximum_fusion.taps
  1.8 76.9 %shard_map.64 = f32[4,64,256]{2,1,0:T(8,128)} custom-call(f32[4,64,256]{2,1,0:T(8,128)} %est.1, bf16[2,16,64,256]{3,2,1,0:T(8,128)(2,1)} %vd.1, f32[2,2,4]{2,1,0:T(2,128)} %scales.1, s32[2,2,4]{2,1,0:T(2,128)} %flags.1, f32[2,6,128]{2,1,0:T(8,128)} %select_maximum_fusion.taps), custom_call_target="tpu_custom_call" | custom-call | tf_op jit(solution)/shard_map/pallas_call | solution.py:491
  78.7 1.7 %copy.14 = f32[4,64,256]{2,1,0:T(8,128)} copy(f32[4,64,256]{2,1,0:T(8,128)} %shard_map.64) | data formatting | bytes 524288
  (5 shorter events, 0.0 us)
Async XLA Ops:
  0.0 0.8 copy-start

commit v2 on v1

--- a/solution.py
+++ b/solution.py
@@ -85,9 +85,9 @@
 
 
 def kernel(
-    sizes, est, vd, scales, flags, taps, out,
+    sizes, est, vd_any, scales, flags, taps, out,
     fg, pk, wk, wl, wr, fb, am, bm, mt, gp, ob, zp,
-    r1, r1z, s2, s2z, r2, r2z, ub, zu, zl, zr, yu, yd, ssem, rsem,
+    r1, r1z, s2, s2z, r2, r2z, ub, zu, zl, zr, yu, yd, vd, dsem, ssem, rsem,
 ):
     ny, nz, views, planes, rows_y, rows_z, own, hw = sizes
     nb = rows_y // hw
@@ -119,6 +119,8 @@
     def sent(src, it, sid, dev):
         rcopy(src, src, it, sid, dev).wait_send()
 
+    load = pltpu.make_async_copy(vd_any, vd, dsem)
+    load.start()
     for ref in (wl, wr, zl, zr, yu, yd, zp):
         ref[...] = jnp.zeros_like(ref)
     for e in (0, nb + 1):
@@ -159,27 +161,33 @@
     group_h = lane_h // (2 * hw)
     side_h = (lane_h // hw) % 2
 
+    blocks = list(range(2, nb)) + [1, nb]
+    order = blocks + [0, nb + 1]
+    own_sl = mine(v)
+    gains = []
+
+    def ag_start(it, e):
+        rcopy(fg.at[e, own_sl], fg.at[e, own_sl], it, ne + e, to_b).start()
+        rcopy(fg.at[e, own_sl], fg.at[e, own_sl], it, e, to_a).start()
+
+    def rims_start(it):
+        @pl.when(has_dn)
+        def _():
+            rcopy(fg.at[nb, own_sl], fg.at[0, own_sl], it, s_yd, to_dn).start()
+
+        @pl.when(has_up)
+        def _():
+            rcopy(fg.at[1, own_sl], fg.at[nb + 1, own_sl], it, s_yu, to_up).start()
+
+    rims_start(0)
+    for e in blocks:
+        ag_start(0, e)
+
     for it in range(ITERS):
-        own_sl = mine(v)
-
-        def ag_start(e):
-            rcopy(fg.at[e, own_sl], fg.at[e, own_sl], it, ne + e, to_b).start()
-            rcopy(fg.at[e, own_sl], fg.at[e, own_sl], it, e, to_a).start()
 
         def ag_forward(e):
             landed(fg.at[e, mine(vb)], it, ne + e, to_b)
             rcopy(fg.at[e, mine(vb)], fg.at[e, mine(vb)], it, 2 * ne + e, to_a).start()
-
-        @pl.when(has_dn)
-        def _():
-            rcopy(fg.at[nb, own_sl], fg.at[0, own_sl], it, s_yd, to_dn).start()
-
-        @pl.when(has_up)
-        def _():
-            rcopy(fg.at[1, own_sl], fg.at[nb + 1, own_sl], it, s_yu, to_up).start()
-
-        for b in range(nb):
-            ag_start(1 + b)
 
         if it == 0:
             for vv in range(views):
@@ -192,12 +200,12 @@
         @pl.when(has_up)
         def _():
             landed(fg.at[0, own_sl], it, s_yd, to_up)
-            ag_start(0)
+            ag_start(it, 0)
 
         @pl.when(has_dn)
         def _():
             landed(fg.at[nb + 1, own_sl], it, s_yu, to_dn)
-            ag_start(nb + 1)
+            ag_start(it, nb + 1)
 
         for e in range(ne):
             packed = jnp.zeros((hw, LANES), F32)
@@ -217,7 +225,7 @@
         def _():
             rcopy(wk, wl, it, s_zr, to_rt).start()
 
-        ag_forward(1)
+        ag_forward(blocks[0])
 
         if it == 0:
             for vv in range(views):
@@ -225,6 +233,17 @@
                     bm.at[vv], 0, taps[1, 3 * vv : 3 * vv + 1, :],
                     taps[1, 3 * vv + 1 : 3 * vv + 2, :], planes, hw,
                 )
+            for vv in range(views):
+                mid = planes // 2 * hw
+                along_z = mt[vv, rows_z // 2 : rows_z // 2 + 1, :rows_z].astype(F32)
+                along_z = jnp.sum(along_z, axis=1, keepdims=True)
+                fwd = am[vv * blk + mid : vv * blk + mid + 1, :].astype(F32)
+                bwd = bm[vv, mid : mid + 1, :].astype(F32)
+                gains.append((
+                    jnp.sum(fwd, axis=1, keepdims=True) * along_z,
+                    1.0 / (jnp.sum(bwd, axis=1, keepdims=True) * along_z),
+                ))
+            load.wait()
 
         @pl.when(has_lf)
         def _():
@@ -239,25 +258,25 @@
         rcopy(pk.at[v], pk.at[v], it, s_p + 1, to_b).start()
         rcopy(pk.at[v], pk.at[v], it, s_p, to_a).start()
 
-        for b in range(1, nb):
-            ag_forward(1 + b)
+        for e in blocks[1:]:
+            ag_forward(e)
         for e in (0, nb + 1):
             when_edge(e, functools.partial(ag_forward, e))
         landed(pk.at[vb], it, s_p + 1, to_b)
         rcopy(pk.at[vb], pk.at[vb], it, s_p + 2, to_a).start()
 
-        for e in range(ne):
+        for e in order:
             def arrivals(e=e):
                 landed(fg.at[e, mine(va)], it, e, to_a)
                 landed(fg.at[e, mine(vc)], it, 2 * ne + e, to_a)
             when_edge(e, arrivals)
+            fb[e * blk : (e + 1) * blk, :rows_z] = fg[e].reshape(blk, rows_z).astype(BF)
         landed(pk.at[va], it, s_p, to_a)
         landed(pk.at[vc], it, s_p + 2, to_a)
 
         @pl.loop(0, ne)
         def _(e):
             base = pl.multiple_of(e * blk, blk)
-            fb[pl.ds(base, blk), :rows_z] = fg[e].reshape(blk, rows_z).astype(BF)
             for x in range(planes):
                 rim = jnp.where(group_h == x % own, pk[x // own, e], 0.0)
                 fb[pl.ds(base + x * hw, hw), rows_z:] = rim.astype(BF)
@@ -279,8 +298,10 @@
                     preferred_element_type=F32,
                 )
                 data = vd[vv, :, pl.ds(pl.multiple_of(b * hw, hw), hw), :].astype(F32)
-                ratio = jnp.where(valid == 1, data.reshape(blk, rows_z) * scale / blurred, 1.0)
-                spread = jnp.dot(ratio.astype(BF), mt[vv], preferred_element_type=F32)
+                ratio = jnp.where(
+                    valid == 1, data.reshape(blk, rows_z) * (scale * gains[vv][0]) / blurred, 1.0
+                )
+                spread = jnp.dot((ratio * gains[vv][1]).astype(BF), mt[vv], preferred_element_type=F32)
                 gp[vv, pl.ds(base + 2 * blk, blk), :] = spread.astype(BF)
 
         @pl.when(has_dn)
@@ -316,18 +337,18 @@
             owner = (va, vc)[k]
             return rcopy(ob.at[e, mine(owner)], r1.at[e, k], it, s_r1 + 2 * e + k, to_a)
 
+        def back(e, lanes):
+            rows = pl.ds(pl.multiple_of(e * blk, blk), 3 * blk)
+            total = jnp.dot(bm[0], gp[0, rows, lanes], preferred_element_type=F32)
+            for vv in range(1, views):
+                total = total + jnp.dot(bm[vv], gp[vv, rows, lanes], preferred_element_type=F32)
+            return total
+
         @pl.loop(0, ne)
         def _(e):
             @pl.when(used(e))
             def _():
-                rows = pl.ds(pl.multiple_of(e * blk, blk), 3 * blk)
-                total = jnp.dot(bm[0], gp[0, rows, :], preferred_element_type=F32)
-                for vv in range(1, views):
-                    total = total + jnp.dot(bm[vv], gp[vv, rows, :], preferred_element_type=F32)
-                ob[e] = total[:, :rows_z].reshape(planes, hw, rows_z)
-                r1_copy(e, 1).start()
-                r1_copy(e, 0).start()
-                rims = total[:, rows_z:].reshape(planes, hw, LANES)
+                rims = back(e, slice(rows_z, None)).reshape(planes, hw, LANES)
                 for o in range(planes // own):
                     packed = rims[own * o]
                     for p in range(1, own):
@@ -337,25 +358,31 @@
         rcopy(zp.at[vc], r1z.at[1], it, s_z + 1, to_a).start()
         rcopy(zp.at[va], r1z.at[0], it, s_z, to_a).start()
 
-        @pl.loop(0, ne)
-        def _(e):
-            @pl.when(used(e))
+        def nth(i):
+            e = jnp.where(i == nb, 1, jnp.where(i == nb + 1, nb, i))
+            return jnp.where(i == 0, 0, jnp.where(i == 1, nb + 1, e))
+
+        @pl.loop(0, ne + 1)
+        def _(i):
+            e = nth(i)
+            @pl.when((i < ne) & used(e))
             def _():
-                r1_copy(e, 1).wait_recv()
-                s2[e] = ob[e, mine(vb)] + r1[e, 1]
-                rcopy(s2.at[e], r2.at[e], it, s_r2 + e, to_b).start()
-
-        landed(r1z.at[1], it, s_z + 1, to_a)
-        s2z[...] = zp[vb] + r1z[1]
-        rcopy(s2z, r2z, it, s_z + 2, to_b).start()
-
-        @pl.loop(0, ne)
-        def _(e):
-            @pl.when(used(e))
+                ob[e] = back(e, slice(0, rows_z)).reshape(planes, hw, rows_z)
+                r1_copy(e, 1).start()
+                r1_copy(e, 0).start()
+
+            @pl.when(i == 1)
             def _():
-                r1_copy(e, 0).wait_recv()
-                landed(r2.at[e], it, s_r2 + e, to_b)
-                ub[e] = ob[e, own_sl] + r1[e, 0] + r2[e]
+                landed(r1z.at[1], it, s_z + 1, to_a)
+                s2z[...] = zp[vb] + r1z[1]
+                rcopy(s2z, r2z, it, s_z + 2, to_b).start()
+
+            q = nth(jnp.maximum(i - 1, 0))
+            @pl.when((i > 0) & used(q))
+            def _():
+                r1_copy(q, 1).wait_recv()
+                s2[q] = ob[q, mine(vb)] + r1[q, 1]
+                rcopy(s2.at[q], r2.at[q], it, s_r2 + q, to_b).start()
 
         landed(r1z.at[0], it, s_z, to_a)
         landed(r2z, it, s_z + 2, to_b)
@@ -369,6 +396,21 @@
         def _():
             rcopy(zu, zl, it, s_rr, to_rt).start()
 
+        def gather_sum(e):
+            r1_copy(e, 0).wait_recv()
+            landed(r2.at[e], it, s_r2 + e, to_b)
+            ub[e] = ob[e, own_sl] + r1[e, 0] + r2[e]
+
+        def add_rims(e):
+            for p in range(own):
+                last = roll_lanes(zr[e], LANES - hw - 2 * hw * p)
+                first = roll_lanes(zl[e], -(2 * hw * p + hw))
+                ub[e, p, :, :LANES] += jnp.where(lane_h < hw, first, 0.0)
+                ub[e, p, :, rows_z - LANES :] += jnp.where(lane_h >= LANES - hw, last, 0.0)
+
+        for e in (0, nb + 1):
+            when_edge(e, functools.partial(gather_sum, e))
+
         @pl.when(has_rt)
         def _():
             landed(zr, it, s_rl, to_rt)
@@ -377,14 +419,8 @@
         def _():
             landed(zl, it, s_rr, to_lf)
 
-        for e in range(ne):
-            def add_rims(e=e):
-                for p in range(own):
-                    last = roll_lanes(zr[e], LANES - hw - 2 * hw * p)
-                    first = roll_lanes(zl[e], -(2 * hw * p + hw))
-                    ub[e, p, :, :LANES] += jnp.where(lane_h < hw, first, 0.0)
-                    ub[e, p, :, rows_z - LANES :] += jnp.where(lane_h >= LANES - hw, last, 0.0)
-            when_edge(e, add_rims)
+        for e in (0, nb + 1):
+            when_edge(e, functools.partial(add_rims, e))
 
         @pl.when(has_up)
         def _():
@@ -394,26 +430,32 @@
         def _():
             rcopy(ub.at[nb + 1], yu, it, s_rd, to_dn).start()
 
-        @pl.when(has_dn)
-        def _():
-            landed(yd, it, s_ru, to_dn)
-
-        @pl.when(has_up)
-        def _():
-            landed(yu, it, s_rd, to_up)
-
-        for b in range(nb):
+        for e in blocks:
+            gather_sum(e)
+            add_rims(e)
+            if e == 1:
+                @pl.when(has_up)
+                def _():
+                    landed(yu, it, s_rd, to_up)
+            if e == nb:
+                @pl.when(has_dn)
+                def _():
+                    landed(yd, it, s_ru, to_dn)
             for p in range(own):
-                total = ub[1 + b, p]
-                if b == 0:
+                total = ub[e, p]
+                if e == 1:
                     total = total + yu[p]
-                if b == nb - 1:
+                if e == nb:
                     total = total + yd[p]
-                fresh = fg[1 + b, own * v + p] * total / view_total
+                fresh = fg[e, own * v + p] * total / view_total
                 if it + 1 < ITERS:
-                    fg[1 + b, own * v + p] = fresh
+                    fg[e, own * v + p] = fresh
                 else:
-                    out[p, b * hw : (b + 1) * hw, :] = fresh
+                    out[p, (e - 1) * hw : e * hw, :] = fresh
+            if it + 1 < ITERS:
+                ag_start(it + 1, e)
+        if it + 1 < ITERS:
+            rims_start(it + 1)
 
         @pl.loop(0, ne)
         def _(e):
@@ -483,6 +525,8 @@
         vm((ne, hw, LANES), F32),
         vm((own, hw, rows_z), F32),
         vm((own, hw, rows_z), F32),
+        vm(view_data.shape, view_data.dtype),
+        pltpu.SemaphoreType.DMA,
         pltpu.SemaphoreType.DMA((ITERS, n_sem)),
         pltpu.SemaphoreType.DMA((ITERS, n_sem)),
     ]
@@ -491,7 +535,7 @@
     return pl.pallas_call(
         functools.partial(kernel, (ny, nz, views, planes, rows_y, rows_z, own, hw)),
         out_shape=jax.ShapeDtypeStruct(estimate.shape, F32),
-        in_specs=[in_vm, in_vm, in_sm, in_sm, in_vm],
+        in_specs=[in_vm, pl.BlockSpec(memory_space=pl.ANY), in_sm, in_sm, in_vm],
         out_specs=in_vm,
         scratch_shapes=scratch,
         compiler_params=pltpu.CompilerParams(collective_id=0, has_side_effects=True),

time: 80.5 us -> 68 us (0.84)
  Pallas kernels: 76.9 us -> 64.4 us
    pallas_call x1, Pallas kernels: 76.9 us -> 64.4 us  [per_device(): pl.pallas_call(functools.partial(kernel, (ny, nz, views, planes, rows_y,...]
where the time goes in v2:
time: 68 us; the launch traced here: 67.8 us
  Pallas kernels  64.4 us (95%)
  local copies, waits for them, and re-layouts  2.57 us (4%)
  other arithmetic  0.85 us (1%)
    pallas_call x1, Pallas kernels, per_device(): pl.pallas_call(functools.partial(kernel, (ny, nz, views, planes, rows_y,...  64.4 us
    unnamed x4, local copies, waits for them, and re-layouts  2.45 us

profile of v2, /device:TPU:0, one launch (start us, length us, event | category | flops | bytes accessed | tf_op | source)
XLA Modules:
  0.0 67.8 jit_solution(5386811077591846470)
XLA Ops:
  0.0 0.0 copy-start
  0.0 0.8 %copy.10 = s32[2,3]{0,1:T(4,128)S(1)} copy(s32[2,3]{1,0:T(2,128)} %param.11) | data formatting | bytes 48 | tf_op args[5]
  0.8 0.0 copy-done
  0.8 0.2 fusion.1
  0.9 0.1 fusion
  1.0 0.1 rev.3
  1.1 0.6 select_maximum_fusion.taps
  1.8 64.4 %shard_map.64 = f32[4,64,256]{2,1,0:T(8,128)} custom-call(f32[4,64,256]{2,1,0:T(8,128)} %est.1, bf16[2,16,64,256]{3,2,1,0:T(8,128)(2,1)} %vd_any.1, f32[2,2,4]{2,1,0:T(2,128)} %scales.1, s32[2,2,4]{2,1,0:T(2,128)} %flags.1, f32[2,6,128]{2,1,0:T(8,128)} %select_maximum_fusion.taps), custom_call_target="tpu_custom_call" | custom-call | tf_op jit(solution)/shard_map/pallas_call | solution.py:535
  66.2 1.7 %copy.14 = f32[4,64,256]{2,1,0:T(8,128)} copy(f32[4,64,256]{2,1,0:T(8,128)} %shard_map.64) | data formatting | bytes 524288
  (5 shorter events, 0.0 us)
Async XLA Ops:
  0.0 0.8 %copy-start = (f32[2,3,33]{2,0,1:T(2,128)S(1)}, f32[2,3,33]{2,0,1:T(2,128)}, u32[]{:S(2)}) copy-start(f32[2,3,33]{2,0,1:T(2,128)} %param.10) | copy-start | bytes 2380

commit v3 on v2

--- a/solution.py
+++ b/solution.py
@@ -87,7 +87,7 @@
 def kernel(
     sizes, est, vd_any, scales, flags, taps, out,
     fg, pk, wk, wl, wr, fb, am, bm, mt, gp, ob, zp,
-    r1, r1z, s2, s2z, r2, r2z, ub, zu, zl, zr, yu, yd, vd, dsem, ssem, rsem,
+    r1, r1z, s2, s2z, r2, r2z, ub, zu, zl, zr, yu, yd, vd, rb, g1, gs, dsem, ssem, rsem,
 ):
     ny, nz, views, planes, rows_y, rows_z, own, hw = sizes
     nb = rows_y // hw
@@ -239,10 +239,14 @@
                 along_z = jnp.sum(along_z, axis=1, keepdims=True)
                 fwd = am[vv * blk + mid : vv * blk + mid + 1, :].astype(F32)
                 bwd = bm[vv, mid : mid + 1, :].astype(F32)
-                gains.append((
-                    jnp.sum(fwd, axis=1, keepdims=True) * along_z,
-                    1.0 / (jnp.sum(bwd, axis=1, keepdims=True) * along_z),
-                ))
+                gain = 1.0 / (jnp.sum(bwd, axis=1, keepdims=True) * along_z)
+                gains.append((jnp.sum(fwd, axis=1, keepdims=True) * along_z, gain))
+                ones = jnp.sum(mt[vv].astype(F32), axis=0, keepdims=True) * gain
+                g1[vv] = jnp.broadcast_to(ones, g1.shape[1:])
+                for j in range(3):
+                    part = bm[vv, :, j * blk : (j + 1) * blk].astype(F32)
+                    part = jnp.sum(part, axis=1, keepdims=True)
+                    rb[vv, j] = jnp.broadcast_to(part, rb.shape[2:])
             load.wait()
 
         @pl.when(has_lf)
@@ -258,19 +262,27 @@
         rcopy(pk.at[v], pk.at[v], it, s_p + 1, to_b).start()
         rcopy(pk.at[v], pk.at[v], it, s_p, to_a).start()
 
-        for e in blocks[1:]:
-            ag_forward(e)
-        for e in (0, nb + 1):
-            when_edge(e, functools.partial(ag_forward, e))
-        landed(pk.at[vb], it, s_p + 1, to_b)
-        rcopy(pk.at[vb], pk.at[vb], it, s_p + 2, to_a).start()
-
-        for e in order:
-            def arrivals(e=e):
+        have = set()
+
+        def process(e):
+            def arrivals():
                 landed(fg.at[e, mine(va)], it, e, to_a)
                 landed(fg.at[e, mine(vc)], it, 2 * ne + e, to_a)
             when_edge(e, arrivals)
             fb[e * blk : (e + 1) * blk, :rows_z] = fg[e].reshape(blk, rows_z).astype(BF)
+            before = {b for b in range(nb) if {b, b + 1, b + 2} <= have}
+            have.add(e)
+            for b in range(nb):
+                if b not in before and {b, b + 1, b + 2} <= have:
+                    core = fb[b * blk : (b + 3) * blk, :rows_z]
+                    gs[b] = jnp.dot(am[...], core, preferred_element_type=F32).astype(BF)
+
+        for k in range(1, ne):
+            when_edge(order[k], functools.partial(ag_forward, order[k]))
+            process(order[k - 1])
+        landed(pk.at[vb], it, s_p + 1, to_b)
+        rcopy(pk.at[vb], pk.at[vb], it, s_p + 2, to_a).start()
+        process(order[-1])
         landed(pk.at[va], it, s_p, to_a)
         landed(pk.at[vc], it, s_p + 2, to_a)
 
@@ -284,7 +296,9 @@
         @pl.loop(0, nb)
         def _(b):
             base = pl.multiple_of(b * blk, blk)
-            g = jnp.dot(am[...], fb[pl.ds(base, 3 * blk), :], preferred_element_type=F32).astype(BF)
+            edge = fb[pl.ds(base, 3 * blk), rows_z:]
+            edge = jnp.dot(am[...], edge, preferred_element_type=F32).astype(BF)
+            g = jnp.concatenate([gs[b], edge], axis=1)
             z_block = lax.broadcasted_iota(jnp.int32, (1, rows_z), 1) // BZ
             y_block = b * hw // BY
             for vv in range(views):
@@ -299,9 +313,9 @@
                 )
                 data = vd[vv, :, pl.ds(pl.multiple_of(b * hw, hw), hw), :].astype(F32)
                 ratio = jnp.where(
-                    valid == 1, data.reshape(blk, rows_z) * (scale * gains[vv][0]) / blurred, 1.0
+                    valid == 1, data.reshape(blk, rows_z) * (scale * gains[vv][0]) / blurred - 1.0, 0.0
                 )
-                spread = jnp.dot((ratio * gains[vv][1]).astype(BF), mt[vv], preferred_element_type=F32)
+                spread = jnp.dot(ratio.astype(BF), mt[vv], preferred_element_type=F32) * gains[vv][1]
                 gp[vv, pl.ds(base + 2 * blk, blk), :] = spread.astype(BF)
 
         @pl.when(has_dn)
@@ -342,6 +356,13 @@
             total = jnp.dot(bm[0], gp[0, rows, lanes], preferred_element_type=F32)
             for vv in range(1, views):
                 total = total + jnp.dot(bm[vv], gp[vv, rows, lanes], preferred_element_type=F32)
+            for vv in range(views):
+                across = jnp.zeros((blk, LANES), F32)
+                for j in range(3):
+                    inside = (e + j >= 2) & (e + j < nb + 2)
+                    across = across + rb[vv, j] * jnp.where(inside, 1.0, 0.0)
+                row = g1[vv, 0:1, lanes]
+                total = total + jnp.concatenate([across] * (row.shape[1] // LANES), axis=1) * row
             return total
 
         @pl.loop(0, ne)
@@ -526,6 +547,9 @@
         vm((own, hw, rows_z), F32),
         vm((own, hw, rows_z), F32),
         vm(view_data.shape, view_data.dtype),
+        vm((views, 3, blk, LANES), F32),
+        vm((views, 8, wide), F32),
+        vm((nb, views * blk, rows_z), BF),
         pltpu.SemaphoreType.DMA,
         pltpu.SemaphoreType.DMA((ITERS, n_sem)),
         pltpu.SemaphoreType.DMA((ITERS, n_sem)),

time: 68 us -> 69.8 us (1.026)
  Pallas kernels: 64.4 us -> 66.2 us
    pallas_call x1, Pallas kernels: 64.4 us -> 66.2 us  [per_device(): pl.pallas_call(functools.partial(kernel, (ny, nz, views, planes, rows_y,...]
where the time goes in v3:
time: 69.8 us; the launch traced here: 69.6 us
  Pallas kernels  66.2 us (95%)
  local copies, waits for them, and re-layouts  2.57 us (4%)
  other arithmetic  0.85 us (1%)
    pallas_call x1, Pallas kernels, per_device(): pl.pallas_call(functools.partial(kernel, (ny, nz, views, planes, rows_y,...  66.2 us
    unnamed x4, local copies, waits for them, and re-layouts  2.45 us

profile of v3, /device:TPU:0, one launch (start us, length us, event | category | flops | bytes accessed | tf_op | source)
XLA Modules:
  0.0 69.6 jit_solution(3491374905648412660)
XLA Ops:
  0.0 0.0 copy-start
  0.0 0.8 %copy.10 = s32[2,3]{0,1:T(4,128)S(1)} copy(s32[2,3]{1,0:T(2,128)} %param.11) | data formatting | bytes 48 | tf_op args[5]
  0.8 0.0 copy-done
  0.8 0.2 fusion.1
  0.9 0.1 fusion
  1.0 0.1 rev.3
  1.1 0.6 select_maximum_fusion.taps
  1.8 66.2 %shard_map.64 = f32[4,64,256]{2,1,0:T(8,128)} custom-call(f32[4,64,256]{2,1,0:T(8,128)} %est.1, bf16[2,16,64,256]{3,2,1,0:T(8,128)(2,1)} %vd_any.1, f32[2,2,4]{2,1,0:T(2,128)} %scales.1, s32[2,2,4]{2,1,0:T(2,128)} %flags.1, f32[2,6,128]{2,1,0:T(8,128)} %select_maximum_fusion.taps), custom_call_target="tpu_custom_call" | custom-call | tf_op jit(solution)/shard_map/pallas_call | solution.py:559
  67.9 1.7 %copy.14 = f32[4,64,256]{2,1,0:T(8,128)} copy(f32[4,64,256]{2,1,0:T(8,128)} %shard_map.64) | data formatting | bytes 524288
  (5 shorter events, 0.0 us)
Async XLA Ops:
  0.0 0.8 %copy-start = (f32[2,3,33]{2,0,1:T(2,128)S(1)}, f32[2,3,33]{2,0,1:T(2,128)}, u32[]{:S(2)}) copy-start(f32[2,3,33]{2,0,1:T(2,128)} %param.10) | copy-start | bytes 2380

commit v4 on v3

--- a/solution.py
+++ b/solution.py
@@ -227,27 +227,6 @@
 
         ag_forward(blocks[0])
 
-        if it == 0:
-            for vv in range(views):
-                build_plane_row(
-                    bm.at[vv], 0, taps[1, 3 * vv : 3 * vv + 1, :],
-                    taps[1, 3 * vv + 1 : 3 * vv + 2, :], planes, hw,
-                )
-            for vv in range(views):
-                mid = planes // 2 * hw
-                along_z = mt[vv, rows_z // 2 : rows_z // 2 + 1, :rows_z].astype(F32)
-                along_z = jnp.sum(along_z, axis=1, keepdims=True)
-                fwd = am[vv * blk + mid : vv * blk + mid + 1, :].astype(F32)
-                bwd = bm[vv, mid : mid + 1, :].astype(F32)
-                gain = 1.0 / (jnp.sum(bwd, axis=1, keepdims=True) * along_z)
-                gains.append((jnp.sum(fwd, axis=1, keepdims=True) * along_z, gain))
-                ones = jnp.sum(mt[vv].astype(F32), axis=0, keepdims=True) * gain
-                g1[vv] = jnp.broadcast_to(ones, g1.shape[1:])
-                for j in range(3):
-                    part = bm[vv, :, j * blk : (j + 1) * blk].astype(F32)
-                    part = jnp.sum(part, axis=1, keepdims=True)
-                    rb[vv, j] = jnp.broadcast_to(part, rb.shape[2:])
-            load.wait()
 
         @pl.when(has_lf)
         def _():
@@ -261,6 +240,36 @@
             pk[v, e] = jnp.where(side_h == 0, wl[e], wr[e])
         rcopy(pk.at[v], pk.at[v], it, s_p + 1, to_b).start()
         rcopy(pk.at[v], pk.at[v], it, s_p, to_a).start()
+
+        def build_back(vv):
+            build_plane_row(
+                bm.at[vv], 0, taps[1, 3 * vv : 3 * vv + 1, :],
+                taps[1, 3 * vv + 1 : 3 * vv + 2, :], planes, hw,
+            )
+
+        def sum_tables(vv):
+            mid = planes // 2 * hw
+            along_z = mt[vv, rows_z // 2 : rows_z // 2 + 1, :rows_z].astype(F32)
+            along_z = jnp.sum(along_z, axis=1, keepdims=True)
+            fwd = am[vv * blk + mid : vv * blk + mid + 1, :].astype(F32)
+            bwd = bm[vv, mid : mid + 1, :].astype(F32)
+            gain = 1.0 / (jnp.sum(bwd, axis=1, keepdims=True) * along_z)
+            gains.append((jnp.sum(fwd, axis=1, keepdims=True) * along_z, gain))
+            ones = jnp.sum(mt[vv].astype(F32), axis=0, keepdims=True) * gain
+            g1[vv] = jnp.broadcast_to(ones, g1.shape[1:])
+            parts = []
+            for j in range(3):
+                part = bm[vv, :, j * blk : (j + 1) * blk].astype(F32)
+                part = jnp.sum(part, axis=1, keepdims=True)
+                parts.append(jnp.broadcast_to(part, rb.shape[2:]))
+            for e in range(ne):
+                rb[e, vv] = sum(parts[j] for j in range(3) if 2 <= e + j < nb + 2)
+
+        tasks = []
+        if it == 0:
+            for vv in range(views):
+                tasks.append(functools.partial(build_back, vv))
+                tasks.append(functools.partial(sum_tables, vv))
 
         have = set()
 
@@ -280,6 +289,12 @@
         for k in range(1, ne):
             when_edge(order[k], functools.partial(ag_forward, order[k]))
             process(order[k - 1])
+            if tasks:
+                tasks.pop(0)()
+        for task in tasks:
+            task()
+        if it == 0:
+            load.wait()
         landed(pk.at[vb], it, s_p + 1, to_b)
         rcopy(pk.at[vb], pk.at[vb], it, s_p + 2, to_a).start()
         process(order[-1])
@@ -357,10 +372,7 @@
             for vv in range(1, views):
                 total = total + jnp.dot(bm[vv], gp[vv, rows, lanes], preferred_element_type=F32)
             for vv in range(views):
-                across = jnp.zeros((blk, LANES), F32)
-                for j in range(3):
-                    inside = (e + j >= 2) & (e + j < nb + 2)
-                    across = across + rb[vv, j] * jnp.where(inside, 1.0, 0.0)
+                across = rb[e, vv]
                 row = g1[vv, 0:1, lanes]
                 total = total + jnp.concatenate([across] * (row.shape[1] // LANES), axis=1) * row
             return total
@@ -547,7 +559,7 @@
         vm((own, hw, rows_z), F32),
         vm((own, hw, rows_z), F32),
         vm(view_data.shape, view_data.dtype),
-        vm((views, 3, blk, LANES), F32),
+        vm((ne, views, blk, LANES), F32),
         vm((views, 8, wide), F32),
         vm((nb, views * blk, rows_z), BF),
         pltpu.SemaphoreType.DMA,

time: 69.8 us -> 69.7 us (level)
  no operation moved by 1% of the time
where the time goes in v4:
time: 69.7 us; the launch traced here: 69.5 us
  Pallas kernels  66.1 us (95%)
  local copies, waits for them, and re-layouts  2.57 us (4%)
  other arithmetic  0.85 us (1%)
    pallas_call x1, Pallas kernels, per_device(): pl.pallas_call(functools.partial(kernel, (ny, nz, views, planes, rows_y,...  66.1 us
    unnamed x4, local copies, waits for them, and re-layouts  2.45 us

profile of v4, /device:TPU:0, one launch (start us, length us, event | category | flops | bytes accessed | tf_op | source)
XLA Modules:
  0.0 69.5 jit_solution(2476533202195570293)
XLA Ops:
  0.0 0.0 copy-start
  0.0 0.8 %copy.10 = s32[2,3]{0,1:T(4,128)S(1)} copy(s32[2,3]{1,0:T(2,128)} %param.11) | data formatting | bytes 48 | tf_op args[5]
  0.8 0.0 copy-done
  0.8 0.2 fusion.1
  0.9 0.1 fusion
  1.0 0.1 rev.3
  1.1 0.6 select_maximum_fusion.taps
  1.8 66.1 %shard_map.64 = f32[4,64,256]{2,1,0:T(8,128)} custom-call(f32[4,64,256]{2,1,0:T(8,128)} %est.1, bf16[2,16,64,256]{3,2,1,0:T(8,128)(2,1)} %vd_any.1, f32[2,2,4]{2,1,0:T(2,128)} %scales.1, s32[2,2,4]{2,1,0:T(2,128)} %flags.1, f32[2,6,128]{2,1,0:T(8,128)} %select_maximum_fusion.taps), custom_call_target="tpu_custom_call" | custom-call | tf_op jit(solution)/shard_map/pallas_call | solution.py:571
  67.9 1.7 %copy.14 = f32[4,64,256]{2,1,0:T(8,128)} copy(f32[4,64,256]{2,1,0:T(8,128)} %shard_map.64) | data formatting | bytes 524288
  (5 shorter events, 0.0 us)
Async XLA Ops:
  0.0 0.8 %copy-start = (f32[2,3,33]{2,0,1:T(2,128)S(1)}, f32[2,3,33]{2,0,1:T(2,128)}, u32[]{:S(2)}) copy-start(f32[2,3,33]{2,0,1:T(2,128)} %param.10) | copy-start | bytes 2380
